TPU v7x, 256 devices: a whole 4x4x8 slice. The times are simulated.
256 devices in a mesh: case: 4 (over y_hi, core), mod: 64 (over x, y_lo, z).
Axes of the slice: x: 4, y: 4 (y_hi: 2, y_lo: 2; y = y_hi * 2 + y_lo), z: 8, core: 2. Of those that a mesh axis runs over, the one named last changes fastest.
Arguments:
- turbulence: float32 [4, 256, 256], P('case'), may hold values from -6 to 6
- pupil_amp: float32 [256, 256], replicated, may hold values from 0.3 to 1
- mod_points: int32 [64], P('mod'), may hold values from 0 to 255
- valid_pix: int32 [65536], P('mod'), may hold values from 0 to 262143, as said below
- recon: bfloat16 [5120, 65536], P('case', 'mod'), may hold values from -0.0234375 to 0.0234375
- gx: float32 [256, 64], replicated, may hold values from -1.2 to 1.2
- gy: float32 [256, 80], replicated, may hold values from -1.2 to 1.2
- act_map: int32 [5120], replicated, may hold values from 0 to 5119, each once
Outputs:
- command_total: float32 [4, 5120], P('case')
- frame: float32 [4, 512, 512], P('case', 'mod')
Inputs may be any that keep to these rules, and one draw needn't show every extreme that they name: `valid_pix`: entries k * 1024 to (k + 1) * 1024 - 1 are flat indices (row times 512 plus column) of pixels in detector rows k * 8 to (k + 1) * 8 - 1.
All inputs are finite; a program needn't handle non-finite values.
Results may differ from a plain program's by a relative error of at most 0.0058.
Values may be sent and summed in bfloat16 or wider, within the bound.
A program may use at most 64 MiB of HBM per device.

v0:
```python
import math

import jax
import jax.numpy as jnp
from jax import lax
from jax.sharding import PartitionSpec as P

STEPS = 2


loop_gain = 0.5
radius_pixels = 6.0
point_count = 256


def phase_table(length, pupil_width, sign_factor):
    centred = jnp.arange(length, dtype=jnp.int32) - length // 2
    position = jnp.arange(pupil_width, dtype=jnp.int32)
    wrapped = jnp.mod(centred[:, None] * position[None, :], length).astype(jnp.float32)
    angles = 2.0 * math.pi / length * wrapped
    factor = 1.0 / math.sqrt(length)
    return (jnp.cos(angles) * factor, sign_factor * jnp.sin(angles) * factor)


def optics_tables(pupil_size, length):
    fwd_cos, fwd_sin = phase_table(length, pupil_size, -1.0)
    inv_cos, inv_sin = phase_table(length, length, 1.0)
    inv_cos = inv_cos.T
    inv_sin = inv_sin.T
    table_one = jnp.concatenate([fwd_cos, fwd_sin], 0).astype(jnp.bfloat16)
    table_two = jnp.concatenate(
        [jnp.concatenate([fwd_cos.T, fwd_sin.T], 1), jnp.concatenate([-fwd_sin.T, fwd_cos.T], 1)], 0
    ).astype(jnp.bfloat16)
    table_three = jnp.concatenate([inv_cos, inv_sin], 0).astype(jnp.bfloat16)
    table_four = jnp.concatenate(
        [jnp.concatenate([inv_cos.T, inv_sin.T], 1), jnp.concatenate([-inv_sin.T, inv_cos.T], 1)], 0
    ).astype(jnp.bfloat16)
    offset = jnp.abs(jnp.arange(length, dtype=jnp.float32) - length // 2)
    mask_angle = 0.5 * math.pi * (offset[:, None] + offset[None, :])
    return (table_one, table_two, table_three, table_four, jnp.cos(mask_angle), jnp.sin(mask_angle))


def detector_frame(pupil_phase, amplitude, mod_point, tables):
    table_one, table_two, table_three, table_four, mask_cos, mask_sin = tables
    pupil_size = pupil_phase.shape[0]
    length = mask_cos.shape[0]
    centred = jnp.arange(pupil_size, dtype=jnp.float32) - pupil_size // 2
    tilt_angle = 2.0 * math.pi / point_count * mod_point.astype(jnp.float32)
    tilt_phase = (
        2.0
        * math.pi
        * radius_pixels
        / length
        * (centred[:, None] * jnp.cos(tilt_angle) + centred[None, :] * jnp.sin(tilt_angle))
    )
    total_phase = pupil_phase + tilt_phase
    pupil_field = jnp.concatenate(
        [amplitude * jnp.cos(total_phase), amplitude * jnp.sin(total_phase)], 1
    ).astype(jnp.bfloat16)
    section_one = jnp.dot(table_one, pupil_field, preferred_element_type=jnp.float32)
    real_part = section_one[:length, :pupil_size] - section_one[length:, pupil_size:]
    imag_part = section_one[:length, pupil_size:] + section_one[length:, :pupil_size]
    focal_half = jnp.concatenate([real_part, imag_part], 1).astype(jnp.bfloat16)
    focal_field = jnp.dot(focal_half, table_two, preferred_element_type=jnp.float32)
    focal_real = focal_field[:, :length]
    focal_imag = focal_field[:, length:]
    masked = jnp.concatenate(
        [
            focal_real * mask_cos - focal_imag * mask_sin,
            focal_real * mask_sin + focal_imag * mask_cos,
        ],
        1,
    ).astype(jnp.bfloat16)
    section_three = jnp.dot(table_three, masked, preferred_element_type=jnp.float32)
    inverse_half = jnp.concatenate(
        [
            section_three[:length, :length] - section_three[length:, length:],
            section_three[:length, length:] + section_three[length:, :length],
        ],
        1,
    ).astype(jnp.bfloat16)
    detector_field = jnp.dot(inverse_half, table_four, preferred_element_type=jnp.float32)
    return detector_field[:, :length] ** 2 + detector_field[:, length:] ** 2


def mirror_surface(commands, act_map, gx, gy):
    actuator_grid = commands[act_map].reshape(gx.shape[1], gy.shape[1])
    rows_mapped = jnp.dot(
        gx, actuator_grid, precision=lax.Precision.HIGHEST, preferred_element_type=jnp.float32
    )
    return jnp.dot(
        rows_mapped, gy.T, precision=lax.Precision.HIGHEST, preferred_element_type=jnp.float32
    )


def body(turbulence, pupil_amp, mod_points, valid_pix, recon, gx, gy, act_map):
    pupil_size = pupil_amp.shape[0]
    length = 2 * pupil_size
    tables = optics_tables(pupil_size, length)
    screen = turbulence[0]
    mod_point = mod_points[0]
    devices_mod = lax.axis_size("mod")
    row_count = length // devices_mod
    command_total = jnp.zeros((1, act_map.shape[0]), jnp.float32)
    pupil_phase = screen
    frame_block = jnp.zeros((row_count, length), jnp.float32)
    for iteration in range(STEPS):
        frame_term = detector_frame(pupil_phase, pupil_amp, mod_point, tables) / devices_mod
        summed = lax.psum(frame_term, "mod")
        frame_block = lax.dynamic_slice_in_dim(
            summed, lax.axis_index("mod") * row_count, row_count, 0
        )
        local_index = valid_pix - lax.axis_index("mod") * (row_count * length)
        signal = frame_block.reshape(-1)[local_index].astype(jnp.bfloat16)
        signals = lax.all_gather(signal[None, :], "case", axis=0, tiled=True)
        partial_commands = lax.dot_general(
            signals, recon, (((1,), (1,)), ((), ())), preferred_element_type=jnp.float32
        )
        summed_commands = lax.psum(partial_commands, "mod")
        own_commands = lax.all_to_all(
            summed_commands, "case", split_axis=0, concat_axis=1, tiled=True
        )
        command_total = command_total + loop_gain * own_commands
        if iteration + 1 < STEPS:
            pupil_phase = screen - mirror_surface(command_total[0], act_map, gx, gy)
    return (command_total, frame_block[None])


def solution(mesh):
    return jax.shard_map(
        body,
        mesh=mesh,
        in_specs=(P("case", None, None), P(), P("mod"), P("mod"), P("case", "mod"), P(), P(), P()),
        out_specs=(P("case", None), P("case", "mod", None)),
        check_vma=False,
    )
```

profile of v0, /device:TPU:1, one launch (start us, length us, event | category | flops | bytes accessed | tf_op | source)
XLA Modules:
  0.0 1675.0 jit_solution(15463527894372798279)
XLA Ops:
  8.2 3.1 multiply_convert_fusion.5
  11.3 3.1 fusion.64
  14.4 9.8 fusion.39
  26.6 1.5 fusion.66
  29.0 4.7 subtract_convert_fusion.1
  33.7 1.3 fusion.15
  38.9 267.6 %all-reduce.4 = bf16[512,512]{1,0:T(8,128)(2,1)} all-reduce(f32[512,512]{1,0:T(8,128)} %fusion.12), channel_id=1, replica_groups=mesh['case'=4,'mod'=64] {'mod'}, use_global_device_ids=true, to_apply=%region_0.1 | all-reduce | flops 262144 | bytes 1572864 | tf_op jit(solution)/shard_map/psum | solution.py:109
  307.3 6.8 gather_fusion
  314.1 62.2 %all-gather = bf16[4096]{0:T(1024)(128)(2,1)S(1)} all-gather(bf16[1024]{0:T(1024)(128)(2,1)S(1)} %gather_fusion), channel_id=2, replica_groups=mesh['case'=4,'mod'=64] {'case'}, dimensions={0}, use_global_device_ids=true | all-gather | bytes 10240 | tf_op jit(solution)/shard_map/all_gather | solution.py:115
  377.1 247.9 %psum.29 = f32[4,1,1280]{2,0,1:T(4,128)S(1)} all-reduce(f32[4,1,1280]{2,0,1:T(4,128)S(1)} %convolution_bitcast_fusion.1), channel_id=1, replica_groups=mesh['case'=4,'mod'=64] {'mod'}, use_global_device_ids=true, to_apply=%region_1.2 | all-reduce | flops 5120 | bytes 40960 | tf_op jit(solution)/shard_map/psum | solution.py:119
  625.6 59.2 %all-to-all-start = ((f32[4,1,1280]{2,1,0:T(1,128)}), f32[4,1,1280]{2,1,0:T(1,128)S(1)}, u32[]{:S(2)}, u32[]{:S(2)}) async-start(f32[4,1,1280]{2,1,0:T(1,128)} %copy.23), calls=%async_computation | async-start | bytes 40960 | tf_op jit(solution)/shard_map/all_to_all | solution.py:120
  684.8 4.6 all-to-all-done
  689.4 28.7 %gather_fusion.1 = f32[5120]{0:T(1024)S(1)} fusion(f32[5120]{0:T(1024)S(1)} %bitcast.31, s32[5120]{0:T(1024)S(1)} %fusion.73), kind=kCustom, calls=%fused_computation.1 | custom fusion | bytes 61440 | tf_op jit(solution)/shard_map/gather | solution.py:87
  719.3 2.2 multiply_convert_fusion.7
  721.6 1.5 fusion.65
  724.0 4.7 subtract_convert_fusion
  728.7 1.3 fusion.23
  733.9 554.2 %all-reduce.3.cloned.1.call-done = f32[512,512]{1,0:T(8,128)} async-done(((f32[512,512]{1,0:T(8,128)}), f32[512,512]{1,0:T(8,128)}) %all-reduce.3.cloned.1.call-update) | async-done | bytes 1048592 | tf_op jit(solution)/shard_map/psum | solution.py:109
  1288.8 6.8 gather_fusion.2
  1295.6 54.1 %all-gather.1 = bf16[4096]{0:T(1024)(128)(2,1)S(1)} all-gather(bf16[1024]{0:T(1024)(128)(2,1)S(1)} %gather_fusion.2), channel_id=3, replica_groups=mesh['case'=4,'mod'=64] {'case'}, dimensions={0}, use_global_device_ids=true | all-gather | bytes 10240 | tf_op jit(solution)/shard_map/all_gather | solution.py:115
  1350.5 252.5 %psum.31 = f32[4,1,1280]{2,0,1:T(4,128)S(1)} all-reduce(f32[4,1,1280]{2,0,1:T(4,128)S(1)} %convolution_bitcast_fusion), channel_id=1, replica_groups=mesh['case'=4,'mod'=64] {'mod'}, use_global_device_ids=true, to_apply=%region_3.4 | all-reduce | flops 5120 | bytes 40960 | tf_op jit(solution)/shard_map/psum | solution.py:119
  1603.7 59.3 %all-to-all-start.1 = ((f32[4,1,1280]{2,1,0:T(1,128)}), f32[4,1,1280]{2,1,0:T(1,128)S(1)}, u32[]{:S(2)}, u32[]{:S(2)}) async-start(f32[4,1,1280]{2,1,0:T(1,128)} %copy.26), calls=%async_computation.1 | async-start | bytes 40960 | tf_op jit(solution)/shard_map/all_to_all | solution.py:120
  1662.9 1.3 dynamic-slice_bitcast_fusion.1
  1664.2 3.3 all-to-all-done.1
  (74 shorter events, 18.0 us)
Async XLA Ops:
  7.2 369.1 %copy-start = (bf16[1280,1024]{1,0:T(8,128)(2,1)S(1)}, bf16[1280,1024]{1,0:T(8,128)(2,1)}, u32[]{:S(2)}) copy-start(bf16[1280,1024]{1,0:T(8,128)(2,1)} %param.12) | copy-start | bytes 7864324
  7.2 17.0 %copy-start.17 = (f32[1,256,256]{2,1,0:T(8,128)S(1)}, f32[1,256,256]{2,1,0:T(8,128)}, u32[]{:S(2)}) copy-start(f32[1,256,256]{2,1,0:T(8,128)} %param.8) | copy-start | bytes 786436
  26.6 1.7 copy-start.11
  26.6 1.7 copy-start.13
  26.6 1.7 copy-start.15
  29.0 4.7 copy-start.7
  29.0 4.7 copy-start.9
  35.0 1.0 copy-start.1
  35.1 1.2 copy-start.3
  35.1 1.3 copy-start.5
  37.7 269.6 %copy-start.19 = (s32[1024]{0:T(1024)S(1)}, s32[1024]{0:T(1024)}, u32[]{:S(2)}) copy-start(s32[1024]{0:T(1024)} %param.11) | copy-start | bytes 12292
  307.3 377.5 %copy-start.18 = (s32[5120]{0:T(1024)S(1)}, s32[5120]{0:T(1024)}, u32[]{:S(2)}) copy-start(s32[5120]{0:T(1024)} %param.15) | copy-start | bytes 61444
  625.6 63.8 %all-to-all-start = ((f32[4,1,1280]{2,1,0:T(1,128)}), f32[4,1,1280]{2,1,0:T(1,128)S(1)}, u32[]{:S(2)}, u32[]{:S(2)}) async-start(f32[4,1,1280]{2,1,0:T(1,128)} %copy.23), calls=%async_computation | async-start | bytes 40960 | tf_op jit(solution)/shard_map/all_to_all | solution.py:120
  684.8 603.3 %all-reduce.3.cloned.1.call-start = ((), (), s32[]{:S(2)}) async-start(), calls=%async_computation.2 | async-start | bytes 2097152 | tf_op jit(solution)/shard_map/psum | solution.py:109
  721.5 1.7 copy-start.12
  721.5 1.7 copy-start.14
  721.5 1.7 copy-start.16
  724.0 4.7 copy-start.8
  724.0 4.7 copy-start.10
  730.0 1.0 copy-start.2
  730.0 1.2 copy-start.4
  730.0 1.3 copy-start.6
  1603.7 63.9 %all-to-all-start.1 = ((f32[4,1,1280]{2,1,0:T(1,128)}), f32[4,1,1280]{2,1,0:T(1,128)S(1)}, u32[]{:S(2)}, u32[]{:S(2)}) async-start(f32[4,1,1280]{2,1,0:T(1,128)} %copy.26), calls=%async_computation.1 | async-start | bytes 40960 | tf_op jit(solution)/shard_map/all_to_all | solution.py:120
Sparse Core Ops, SparseCore 0:
  734.0 554.0 all-reduce.2
where the time goes:
time: 1680 us
  blocking collectives  884 us (53%)
  waiting for transfers between devices  562 us (33%)
  starting transfers between devices  118 us (7%)
  local copies, waits for them, and re-layouts  49.6 us (3%)
  other arithmetic  30.7 us (2%)
    psum x1, waiting for transfers between devices, body(): summed = lax.psum(frame_term, 'mod')  554 us
    psum x2, blocking collectives, body(): summed_commands = lax.psum(partial_commands, 'mod')  500 us
    psum x1, blocking collectives, body(): summed = lax.psum(frame_term, 'mod')  268 us
    all_to_all x2, starting transfers between devices, body(): lax.all_to_all(summed_commands, 'case', split_axis=0, concat_axis=1, tile...  118 us
    all_gather x2, blocking collectives, body(): signals = lax.all_gather(signal[None, :], 'case', axis=0, tiled=True)  116 us
  transfers between devices with their start and end apart: 3, of which 3 were waited for; matrix products, arithmetic and copies ran while one was open for 0% of the time, Pallas kernels for 0%

commit v1 on v0

v1 whole, which is shorter than its diff:
```python
import functools
import math

import jax
import jax.numpy as jnp
import numpy as np
from jax import lax
from jax.experimental import pallas as pl
from jax.experimental.pallas import tpu as pltpu
from jax.sharding import PartitionSpec as P

STEPS = 2
PUPIL = 256
NF = 512
AY = 64
AX = 80
LOOP_GAIN = 0.5
RADIUS = 6.0
POINTS = 256
NX, NYL, NZ = 4, 2, 8
NCASE = 4
MESH = pl.DeviceIdType.MESH
F32 = jnp.float32
BF16 = jnp.bfloat16


def sensor_tables():
    k = np.arange(NF) - NF // 2
    n = np.arange(PUPIL)
    p = np.arange(NF)
    w = np.exp(-2j * np.pi * np.outer(k, n) / NF) / np.sqrt(NF)
    v = np.exp(2j * np.pi * np.outer(p, k) / NF) / np.sqrt(NF)
    turn = np.array([1, 1j, -1, -1j])[np.abs(k) % 4]
    m = (v * turn) @ w
    rows = np.stack([m.real, m.imag]).astype(np.float32)
    return rows, m.imag.T.astype(np.float32)


def sincos(x):
    k = jnp.floor(x * (2.0 / math.pi) + 0.5)
    r = ((x - k * 1.5703125) - k * 4.837512969970703e-4) - k * 7.549789948768648e-8
    r2 = r * r
    s = r + r * r2 * (-1.6666654611e-1 + r2 * (8.3321608736e-3 + r2 * -1.9515295891e-4))
    c = 1.0 + r2 * (-0.5 + r2 * (4.166664568298827e-2 + r2 * (-1.388731625493765e-3 + r2 * 2.443315711809948e-5)))
    q = k - 4.0 * jnp.floor(k * 0.25)
    odd = (q == 1.0) | (q == 3.0)
    sn = jnp.where(odd, c, s)
    cs = jnp.where(odd, s, c)
    sn = jnp.where(q >= 2.0, -sn, sn)
    cs = jnp.where((q == 1.0) | (q == 2.0), -cs, cs)
    return cs, sn


def kernel(
    mod_ref, turb_ref, amp_ref, pix_ref, act_ref, gx_ref, gy_ref, gt_ref, rows_hbm, recon_hbm,
    cmd_out, frame_out,
    recon_ref, rows_ref, mod_a, mod_b, v_ref, l_ref, e_ref, x_ref, t_ref, y_ref,
    oh_sig, oh_act, fr_ref, sig_buf, part_ref, part_bf, plane_buf, tot_ref, z_buf, gat_ref, grid_ref,
    local_sem, send_sem, recv_sem,
):
    c = lax.axis_index("case")
    m = lax.axis_index("mod")
    z = lax.rem(m, NZ)
    xy = lax.div(m, NZ)
    yl = lax.rem(xy, NYL)
    x = lax.div(xy, NYL)

    plane = [(dx, dy, dc) for dx in range(NX) for dy in range(NYL) for dc in range(NCASE) if (dx, dy, dc) != (0, 0, 0)]

    def plane_device(dx, dy, dc):
        px = lax.rem(x + dx, NX)
        py = lax.rem(yl + dy, NYL)
        pc = lax.rem(c + dc, NCASE)
        return pc, (px * NYL + py) * NZ + z

    def z_device(dz):
        return c, xy * NZ + lax.rem(z + dz, NZ)

    barrier = pltpu.get_barrier_semaphore()
    for d in plane:
        pl.semaphore_signal(barrier, inc=1, device_id=plane_device(*d), device_id_type=MESH)
    for dz in range(1, NZ):
        pl.semaphore_signal(barrier, inc=1, device_id=z_device(dz), device_id_type=MESH)

    rows_copy = pltpu.make_async_copy(rows_hbm.at[:, pl.ds(pl.multiple_of(m * 8, 8), 8), :], rows_ref, local_sem.at[0])
    rows_copy.start()
    recon_copy = pltpu.make_async_copy(recon_hbm, recon_ref, local_sem.at[1])
    recon_copy.start()

    def send(src, dst, phase, device):
        pltpu.make_async_remote_copy(
            src_ref=src, dst_ref=dst, send_sem=send_sem.at[phase], recv_sem=recv_sem.at[phase],
            device_id=device, device_id_type=MESH,
        ).start()

    def await_all(ref, phase):
        pltpu.make_async_remote_copy(
            src_ref=ref, dst_ref=ref, send_sem=send_sem.at[phase], recv_sem=recv_sem.at[phase],
            device_id=z_device(1), device_id_type=MESH,
        ).wait_recv()

    def await_sent(ref, phase):
        pltpu.make_async_remote_copy(
            src_ref=ref, dst_ref=ref, send_sem=send_sem.at[phase], recv_sem=recv_sem.at[phase],
            device_id=z_device(1), device_id_type=MESH,
        ).wait_send()

    mod_a[xy] = jnp.full((1, 128), mod_ref[0], jnp.int32).astype(F32)

    def make_field(r, phase):
        cs, sn = sincos(phase)
        amp = amp_ref[r, :]
        er = (amp * cs).astype(BF16)
        ei = (amp * sn).astype(BF16)
        low = slice(r.start + PUPIL, r.stop + PUPIL)
        e_ref[r, 0:PUPIL] = er
        e_ref[r, PUPIL:] = ei
        e_ref[low, 0:PUPIL] = -ei
        e_ref[low, PUPIL:] = er

    for r0 in range(0, PUPIL, 32):
        r = slice(r0, r0 + 32)
        make_field(r, turb_ref[r, :])

    lane = lax.broadcasted_iota(jnp.int32, (128, 128), 0)
    local = pix_ref[...] - m * (8 * NF)
    pix_r = lax.rem(local, 128)
    pix_q = lax.rem(lax.div(local, 128), 4) * 8 + lax.div(local, NF)
    for s in range(8):
        oh_sig[:, 128 * s:128 * s + 128] = jnp.where(lane == pix_r[s:s + 1, :], 1.0, 0.0).astype(BF16)
    act = act_ref[...]
    act_r = lax.rem(act, 128)
    act_q = lax.div(act, 128)
    for s in range(40):
        oh_act[:, 128 * s:128 * s + 128] = jnp.where(lane == act_r[s:s + 1, :], 1.0, 0.0).astype(BF16)
    part_ref[...] = jnp.zeros_like(part_ref)

    pl.semaphore_wait(barrier, len(plane) + NZ - 1)

    near = [(dx, dy) for dx in range(NX) for dy in range(NYL) if (dx, dy) != (0, 0)]
    for dx, dy in near:
        send(mod_a.at[xy], mod_a.at[xy], 0, plane_device(dx, dy, 0))
    await_all(mod_a.at[pl.ds(0, len(near))], 0)
    for j in range(NX * NYL):
        mod_b[z, j:j + 1, :] = mod_a[j]
    for dz in range(1, NZ):
        send(mod_b.at[z], mod_b.at[z], 1, z_device(dz))
    await_all(mod_b.at[pl.ds(0, NZ - 1)], 1)

    angle = (2.0 * math.pi / POINTS) * mod_b[...].reshape(64, 128)
    ca, sa = sincos(angle)
    centred = lax.broadcasted_iota(jnp.int32, (64, 128), 1).astype(F32)
    scale = 2.0 * math.pi * RADIUS / NF
    rows_copy.wait()
    for h in range(2):
        pos = scale * (centred + (128.0 * h - PUPIL // 2))
        cols = slice(128 * h, 128 * h + 128)
        vr, vi = sincos(pos * sa)
        v_ref[0, :, cols] = vr
        v_ref[1, :, cols] = vi
        ur, ui = sincos(pos * ca)
        for i in range(8):
            mr = rows_ref[0, i:i + 1, cols]
            mi = rows_ref[1, i:i + 1, cols]
            l_ref[64 * i:64 * i + 64, cols] = (mr * ur - mi * ui).astype(BF16)
            l_ref[64 * i:64 * i + 64, 128 * h + PUPIL:128 * h + PUPIL + 128] = (mr * ui + mi * ur).astype(BF16)

    for step in range(STEPS):
        if step > 0:
            total = tot_ref[step - 1]
            high = total.astype(BF16)
            low = (total - high.astype(F32)).astype(BF16)
            picked = jnp.dot(jnp.concatenate([high, low], 0), oh_act[...], preferred_element_type=F32)
            q_iota = lax.broadcasted_iota(jnp.int32, (40, 128), 0)
            for s in range(40):
                cols = slice(128 * s, 128 * s + 128)
                block = picked[0:40, cols] + picked[40:80, cols]
                gat_ref[s:s + 1, :] = jnp.sum(jnp.where(q_iota == act_q[s:s + 1, :], block, 0.0), axis=0, keepdims=True)
            for y8 in range(8):
                s5, t = divmod(AX * y8, 128)
                first = gat_ref[pl.ds(s5, 8, stride=5), :]
                if t + AX <= 128:
                    row = first[:, t:t + AX]
                else:
                    second = gat_ref[pl.ds(s5 + 1, 8, stride=5), :]
                    row = jnp.concatenate([first[:, t:], second[:, :t + AX - 128]], axis=1)
                grid_ref[pl.ds(y8, 8, stride=8), :] = jnp.concatenate([row, jnp.zeros((8, 128 - AX), F32)], axis=1)
            mapped = jnp.dot(gx_ref[...], grid_ref[:, 0:AX], precision=lax.Precision.HIGHEST, preferred_element_type=F32)
            surface = lax.dot_general(
                mapped, gy_ref[...], (((1,), (1,)), ((), ())),
                precision=lax.Precision.HIGHEST, preferred_element_type=F32,
            )
            for r0 in range(0, PUPIL, 32):
                r = slice(r0, r0 + 32)
                make_field(r, turb_ref[r, :] - surface[r, :])

        x_ref[...] = jnp.dot(l_ref[...], e_ref[...], preferred_element_type=F32)
        for i in range(8):
            r = slice(64 * i, 64 * i + 64)
            xr = x_ref[r, 0:PUPIL]
            xi = x_ref[r, PUPIL:]
            vr = v_ref[0]
            vi = v_ref[1]
            tr = xr * vr - xi * vi
            ti = xr * vi + xi * vr
            x_ref[r, 0:PUPIL] = tr
            x_ref[r, PUPIL:] = ti
            t_ref[r, :] = tr.astype(BF16)
            t_ref[64 * i + 512:64 * i + 576, :] = ti.astype(BF16)
        y_ref[...] = jnp.dot(t_ref[...], gt_ref[...], preferred_element_type=F32)
        for i in range(8):
            for q in range(4):
                cols = slice(128 * q, 128 * q + 128)
                src = 128 * (1 - q % 2)
                r = slice(64 * i, 64 * i + 64)
                dr = 0.5 * x_ref[r, src:src + 128] - y_ref[64 * i + 512:64 * i + 576, cols]
                di = 0.5 * x_ref[r, src + PUPIL:src + PUPIL + 128] + y_ref[r, cols]
                fr_ref[i:i + 1, cols] = jnp.sum(dr * dr + di * di, axis=0, keepdims=True) * (1.0 / 64)
        frame = fr_ref[...]
        if step == STEPS - 1:
            frame_out[...] = frame

        stacked = jnp.concatenate([frame[:, 128 * q:128 * q + 128] for q in range(4)], axis=0).astype(BF16)
        picked_sig = jnp.dot(stacked, oh_sig[...], preferred_element_type=F32)
        s_iota = lax.broadcasted_iota(jnp.int32, (32, 128), 0)
        for s in range(8):
            cols = slice(128 * s, 128 * s + 128)
            sig_buf[step, c, :, cols] = jnp.sum(
                jnp.where(s_iota == pix_q[s:s + 1, :], picked_sig[:, cols], 0.0), axis=0, keepdims=True
            )
        base = 2 + 3 * step
        for dc in range(1, NCASE):
            send(sig_buf.at[step, c], sig_buf.at[step, c], base, plane_device(0, 0, dc))
        if step == 0:
            recon_copy.wait()
        await_all(sig_buf.at[step, pl.ds(0, NCASE - 1)], base)

        signals = jnp.concatenate([sig_buf[step, k] for k in range(NCASE)], axis=0).astype(BF16)
        part = lax.dot_general(signals, recon_ref[...], (((1,), (1,)), ((), ())), preferred_element_type=F32)
        for k in range(NCASE):
            for j in range(10):
                part_ref[k, j:j + 1, :] = part[k:k + 1, 128 * j:128 * j + 128]
        part_bf[step] = part_ref[...].astype(BF16)
        plane_buf[step, xy * NCASE + c] = part_bf[step, c]
        for d in plane:
            device = plane_device(*d)
            send(part_bf.at[step, device[0]], plane_buf.at[step, xy * NCASE + c], base + 1, device)
        await_all(plane_buf.at[step, pl.ds(0, len(plane))], base + 1)
        for k in range(NCASE):
            acc = plane_buf[step, k].astype(F32)
            for j in range(1, NX * NYL):
                acc = acc + plane_buf[step, j * NCASE + k].astype(F32)
            tot_ref[step, 10 * k:10 * k + 10, :] = acc[0:10, :]
        z_buf[step, z] = tot_ref[step].astype(BF16)
        for dz in range(1, NZ):
            send(z_buf.at[step, z], z_buf.at[step, z], base + 2, z_device(dz))
        await_all(z_buf.at[step, pl.ds(0, NZ - 1)], base + 2)
        acc = z_buf[step, 0].astype(F32)
        for j in range(1, NZ):
            acc = acc + z_buf[step, j].astype(F32)
        acc = LOOP_GAIN * acc
        if step > 0:
            acc = acc + tot_ref[step - 1]
        tot_ref[step] = acc
        if step == STEPS - 1:
            cmd_out[...] = acc

    await_sent(mod_a.at[pl.ds(0, len(near))], 0)
    await_sent(mod_b.at[pl.ds(0, NZ - 1)], 1)
    for step in range(STEPS):
        base = 2 + 3 * step
        await_sent(sig_buf.at[step, pl.ds(0, NCASE - 1)], base)
        await_sent(plane_buf.at[step, pl.ds(0, len(plane))], base + 1)
        await_sent(z_buf.at[step, pl.ds(0, NZ - 1)], base + 2)


def body(turbulence, pupil_amp, mod_points, valid_pix, recon, gx, gy, act_map):
    rows, gt = sensor_tables()
    vmem = pl.BlockSpec(memory_space=pltpu.VMEM)
    anywhere = pl.BlockSpec(memory_space=pl.ANY)
    command, frame = pl.pallas_call(
        kernel,
        out_shape=(jax.ShapeDtypeStruct((40, 128), F32), jax.ShapeDtypeStruct((8, NF), F32)),
        in_specs=[pl.BlockSpec(memory_space=pltpu.SMEM)] + [vmem] * 7 + [anywhere] * 2,
        out_specs=(vmem, vmem),
        scratch_shapes=[
            pltpu.VMEM((1280, 1024), BF16),
            pltpu.VMEM((2, 8, PUPIL), F32),
            pltpu.VMEM((8, 1, 128), F32),
            pltpu.VMEM((8, 8, 128), F32),
            pltpu.VMEM((2, 64, PUPIL), F32),
            pltpu.VMEM((512, 512), BF16),
            pltpu.VMEM((512, 512), BF16),
            pltpu.VMEM((512, 512), F32),
            pltpu.VMEM((1024, PUPIL), BF16),
            pltpu.VMEM((1024, NF), F32),
            pltpu.VMEM((128, 1024), BF16),
            pltpu.VMEM((128, 5120), BF16),
            pltpu.VMEM((8, NF), F32),
            pltpu.VMEM((STEPS, NCASE, 1, 1024), F32),
            pltpu.VMEM((NCASE, 16, 128), F32),
            pltpu.VMEM((STEPS, NCASE, 16, 128), BF16),
            pltpu.VMEM((STEPS, 32, 16, 128), BF16),
            pltpu.VMEM((STEPS, 40, 128), F32),
            pltpu.VMEM((STEPS, NZ, 40, 128), BF16),
            pltpu.VMEM((40, 128), F32),
            pltpu.VMEM((64, 128), F32),
            pltpu.SemaphoreType.DMA((2,)),
            pltpu.SemaphoreType.DMA((2 + 3 * STEPS,)),
            pltpu.SemaphoreType.DMA((2 + 3 * STEPS,)),
        ],
        compiler_params=pltpu.CompilerParams(
            collective_id=0, has_side_effects=True, vmem_limit_bytes=40 * 1024 * 1024
        ),
    )(
        mod_points, turbulence[0], pupil_amp, valid_pix.reshape(8, 128), act_map.reshape(40, 128), gx, gy,
        jnp.asarray(gt).astype(BF16), jnp.asarray(rows), recon,
    )
    return command.reshape(1, 5120), frame[None]


def solution(mesh):
    return jax.shard_map(
        body,
        mesh=mesh,
        in_specs=(P("case", None, None), P(), P("mod"), P("mod"), P("case", "mod"), P(), P(), P()),
        out_specs=(P("case", None), P("case", "mod", None)),
        check_vma=False,
    )
```

time: 1680 us -> 63.8 us (0.04)
  the two profiles are of different devices: /device:TPU:1 before, /device:TPU:4 now
where the time goes in v1:
time: 63.8 us; the launch traced here: 63.4 us
  Pallas kernels  51.7 us (81%)
  local copies, waits for them, and re-layouts  10.3 us (16%)
  between operations  1.31 us (2%)
    pallas_call x1, Pallas kernels, body(): pl.pallas_call(kernel, out_shape=(jax.ShapeDtypeStruct((40, 128), F32), j...  51.7 us
    unnamed x18, local copies, waits for them, and re-layouts  10.3 us

profile of v1, /device:TPU:4, one launch (start us, length us, event | category | flops | bytes accessed | tf_op | source)
XLA Modules:
  0.0 63.4 jit_solution(11579504519657459224)
XLA Ops:
  1.3 0.9 %copy.12.gx_ref = f32[256,64]{1,0:T(8,128)S(1)} copy(f32[256,64]{0,1:T(8,128)} %param.15) | data formatting | bytes 131072 | tf_op args[5]
  2.2 1.0 %copy.13.gy_ref = f32[256,80]{1,0:T(8,128)S(1)} copy(f32[256,80]{0,1:T(8,128)} %param.16) | data formatting | bytes 163840 | tf_op args[6]
  3.2 0.0 copy-start
  3.2 1.7 %copy-done = bf16[1280,1024]{1,0:T(8,128)(2,1)S(1)} copy-done((bf16[1280,1024]{1,0:T(8,128)(2,1)S(1)}, bf16[1280,1024]{1,0:T(8,128)(2,1)}, u32[]{:S(2)}) %copy-start) | copy-done | bytes 2621464
  4.9 0.0 copy-start.1
  4.9 1.2 %copy-done.1 = f32[2,512,256]{2,1,0:T(8,128)S(1)} copy-done((f32[2,512,256]{2,1,0:T(8,128)S(1)}, f32[2,512,256]{2,1,0:T(8,128)}, u32[]{:S(2)}) %copy-start.1) | copy-done | bytes 1048600
  6.2 0.0 copy-start.2
  6.2 0.9 %copy-done.2 = f32[1,256,256]{2,1,0:T(8,128)S(1)} copy-done((f32[1,256,256]{2,1,0:T(8,128)S(1)}, f32[1,256,256]{2,1,0:T(8,128)}, u32[]{:S(2)}) %copy-start.2) | copy-done | bytes 262168
  7.1 0.0 copy-start.3
  7.1 0.9 %copy-done.3 = f32[256,256]{1,0:T(8,128)S(1)} copy-done((f32[256,256]{1,0:T(8,128)S(1)}, f32[256,256]{1,0:T(8,128)}, u32[]{:S(2)}) %copy-start.3) | copy-done | bytes 262168
  8.1 0.0 copy-start.4
  8.1 0.9 %copy-done.4 = bf16[256,512]{1,0:T(8,128)(2,1)S(1)} copy-done((bf16[256,512]{1,0:T(8,128)(2,1)S(1)}, bf16[256,512]{1,0:T(8,128)(2,1)}, u32[]{:S(2)}) %copy-start.4) | copy-done | bytes 262168
  9.0 0.0 copy-start.5
  9.0 0.7 %copy-done.5 = s32[5120]{0:T(1024)S(1)} copy-done((s32[5120]{0:T(1024)S(1)}, s32[5120]{0:T(1024)}, u32[]{:S(2)}) %copy-start.5) | copy-done | bytes 20504
  9.7 0.0 copy-start.6
  9.8 0.7 %copy-done.6 = s32[1024]{0:T(1024)S(1)} copy-done((s32[1024]{0:T(1024)S(1)}, s32[1024]{0:T(1024)}, u32[]{:S(2)}) %copy-start.6) | copy-done | bytes 4120
  10.4 51.7 %shard_map.113 = (f32[40,128]{1,0:T(8,128)S(1)}, f32[8,512]{1,0:T(8,128)S(1)}) custom-call(s32[1]{0:T(128)S(6)} %copy.16.mod_ref, f32[256,256]{1,0:T(8,128)S(1)} %bitcast.5, f32[256,256]{1,0:T(8,128)S(1)} %copy-done.3, s32[8,128]{1,0:T(8,128)S(1)} %bitcast.9, s32[40,128]{1,0:T(8,128)S(1)} %bitcast.6, f32[256,64]{1,0:T(8,128)S(1)} %copy.12.gx_ref, ...), custom_call_target="tpu_custom_call" | custom-call | tf_op jit(solution)/shard_map/pallas_call | solution.py:281
  62.2 0.6 copy.17
  62.8 0.6 copy.18
Async XLA Ops:
  3.2 1.7 %copy-start = (bf16[1280,1024]{1,0:T(8,128)(2,1)S(1)}, bf16[1280,1024]{1,0:T(8,128)(2,1)}, u32[]{:S(2)}) copy-start(bf16[1280,1024]{1,0:T(8,128)(2,1)} %recon_hbm.1) | copy-start | bytes 7864324
  4.9 1.2 %copy-start.1 = (f32[2,512,256]{2,1,0:T(8,128)S(1)}, f32[2,512,256]{2,1,0:T(8,128)}, u32[]{:S(2)}) copy-start(f32[2,512,256]{2,1,0:T(8,128)} %constant.5.clone.rows_hbm) | copy-start | bytes 3145732
  6.2 0.9 %copy-start.2 = (f32[1,256,256]{2,1,0:T(8,128)S(1)}, f32[1,256,256]{2,1,0:T(8,128)}, u32[]{:S(2)}) copy-start(f32[1,256,256]{2,1,0:T(8,128)} %param.10) | copy-start | bytes 786436
  7.1 0.9 %copy-start.3 = (f32[256,256]{1,0:T(8,128)S(1)}, f32[256,256]{1,0:T(8,128)}, u32[]{:S(2)}) copy-start(f32[256,256]{1,0:T(8,128)} %amp_ref.1) | copy-start | bytes 786436
  8.1 0.9 %copy-start.4 = (bf16[256,512]{1,0:T(8,128)(2,1)S(1)}, bf16[256,512]{1,0:T(8,128)(2,1)}, u32[]{:S(2)}) copy-start(bf16[256,512]{1,0:T(8,128)(2,1)} %constant.8.gt_ref) | copy-start | bytes 786436
  9.0 0.7 %copy-start.5 = (s32[5120]{0:T(1024)S(1)}, s32[5120]{0:T(1024)}, u32[]{:S(2)}) copy-start(s32[5120]{0:T(1024)} %param.17) | copy-start | bytes 61444
  9.7 0.7 %copy-start.6 = (s32[1024]{0:T(1024)S(1)}, s32[1024]{0:T(1024)}, u32[]{:S(2)}) copy-start(s32[1024]{0:T(1024)} %param.13) | copy-start | bytes 12292

commit v2 on v1

--- a/solution.py
+++ b/solution.py
@@ -51,9 +51,15 @@
     return cs, sn
 
 
+def halves(x):
+    high = x.astype(BF16)
+    return high, (x - high.astype(F32)).astype(BF16)
+
+
 def kernel(
-    mod_ref, turb_ref, amp_ref, pix_ref, act_ref, gx_ref, gy_ref, gt_ref, rows_hbm, recon_hbm,
+    mod_ref, turb_hbm, amp_hbm, pix_hbm, act_hbm, gx_hbm, gy_hbm, gt_hbm, rows_hbm, recon_hbm,
     cmd_out, frame_out,
+    turb_ref, amp_ref, pix_ref, act_ref, gx_ref, gy_ref, gt_ref, gx_wide, gy_tall,
     recon_ref, rows_ref, mod_a, mod_b, v_ref, l_ref, e_ref, x_ref, t_ref, y_ref,
     oh_sig, oh_act, fr_ref, sig_buf, part_ref, part_bf, plane_buf, tot_ref, z_buf, gat_ref, grid_ref,
     local_sem, send_sem, recv_sem,
@@ -82,10 +88,17 @@
     for dz in range(1, NZ):
         pl.semaphore_signal(barrier, inc=1, device_id=z_device(dz), device_id_type=MESH)
 
-    rows_copy = pltpu.make_async_copy(rows_hbm.at[:, pl.ds(pl.multiple_of(m * 8, 8), 8), :], rows_ref, local_sem.at[0])
-    rows_copy.start()
-    recon_copy = pltpu.make_async_copy(recon_hbm, recon_ref, local_sem.at[1])
-    recon_copy.start()
+    loads = [
+        pltpu.make_async_copy(src, dst, local_sem.at[i])
+        for i, (src, dst) in enumerate((
+            (turb_hbm, turb_ref), (amp_hbm, amp_ref), (pix_hbm, pix_ref), (act_hbm, act_ref),
+            (rows_hbm.at[:, pl.ds(pl.multiple_of(m * 8, 8), 8), :], rows_ref), (gt_hbm, gt_ref),
+            (gx_hbm, gx_ref), (gy_hbm, gy_ref), (recon_hbm, recon_ref),
+        ))
+    ]
+    for load in loads:
+        load.start()
+    turb_load, amp_load, pix_load, act_load, rows_load, gt_load, gx_load, gy_load, recon_load = loads
 
     def send(src, dst, phase, device):
         pltpu.make_async_remote_copy(
@@ -118,22 +131,40 @@
         e_ref[low, 0:PUPIL] = -ei
         e_ref[low, PUPIL:] = er
 
+    turb_load.wait()
+    amp_load.wait()
     for r0 in range(0, PUPIL, 32):
         r = slice(r0, r0 + 32)
         make_field(r, turb_ref[r, :])
 
     lane = lax.broadcasted_iota(jnp.int32, (128, 128), 0)
+    pix_load.wait()
     local = pix_ref[...] - m * (8 * NF)
     pix_r = lax.rem(local, 128)
     pix_q = lax.rem(lax.div(local, 128), 4) * 8 + lax.div(local, NF)
     for s in range(8):
         oh_sig[:, 128 * s:128 * s + 128] = jnp.where(lane == pix_r[s:s + 1, :], 1.0, 0.0).astype(BF16)
+    act_load.wait()
     act = act_ref[...]
     act_r = lax.rem(act, 128)
     act_q = lax.div(act, 128)
     for s in range(40):
         oh_act[:, 128 * s:128 * s + 128] = jnp.where(lane == act_r[s:s + 1, :], 1.0, 0.0).astype(BF16)
     part_ref[...] = jnp.zeros_like(part_ref)
+    grid_ref[...] = jnp.zeros_like(grid_ref)
+
+    gx_load.wait()
+    gx_high, gx_low = halves(gx_ref[...].T)
+    gx_wide[:, 0:AY] = gx_high
+    gx_wide[:, AY:2 * AY] = gx_low
+    gx_wide[:, 2 * AY:] = gx_high
+    gy_load.wait()
+    gy_high, gy_low = halves(gy_ref[...])
+    gy_tall[...] = jnp.zeros_like(gy_tall)
+    gy_tall[0:AX, :] = gy_high
+    gy_tall[128:128 + AX, :] = gy_high
+    gy_tall[256:256 + AX, :] = gy_low
+    gt_load.wait()
 
     pl.semaphore_wait(barrier, len(plane) + NZ - 1)
 
@@ -151,7 +182,7 @@
     ca, sa = sincos(angle)
     centred = lax.broadcasted_iota(jnp.int32, (64, 128), 1).astype(F32)
     scale = 2.0 * math.pi * RADIUS / NF
-    rows_copy.wait()
+    rows_load.wait()
     for h in range(2):
         pos = scale * (centred + (128.0 * h - PUPIL // 2))
         cols = slice(128 * h, 128 * h + 128)
@@ -168,8 +199,7 @@
     for step in range(STEPS):
         if step > 0:
             total = tot_ref[step - 1]
-            high = total.astype(BF16)
-            low = (total - high.astype(F32)).astype(BF16)
+            high, low = halves(total)
             picked = jnp.dot(jnp.concatenate([high, low], 0), oh_act[...], preferred_element_type=F32)
             q_iota = lax.broadcasted_iota(jnp.int32, (40, 128), 0)
             for s in range(40):
@@ -185,10 +215,14 @@
                     second = gat_ref[pl.ds(s5 + 1, 8, stride=5), :]
                     row = jnp.concatenate([first[:, t:], second[:, :t + AX - 128]], axis=1)
                 grid_ref[pl.ds(y8, 8, stride=8), :] = jnp.concatenate([row, jnp.zeros((8, 128 - AX), F32)], axis=1)
-            mapped = jnp.dot(gx_ref[...], grid_ref[:, 0:AX], precision=lax.Precision.HIGHEST, preferred_element_type=F32)
-            surface = lax.dot_general(
-                mapped, gy_ref[...], (((1,), (1,)), ((), ())),
-                precision=lax.Precision.HIGHEST, preferred_element_type=F32,
+            grid_high, grid_low = halves(grid_ref[...])
+            mapped = jnp.dot(
+                jnp.concatenate([grid_high, grid_low, grid_high], axis=1), gy_tall[...], preferred_element_type=F32
+            )
+            mapped_high, mapped_low = halves(mapped)
+            surface = jnp.dot(
+                gx_wide[...], jnp.concatenate([mapped_high, mapped_high, mapped_low], axis=0),
+                preferred_element_type=F32,
             )
             for r0 in range(0, PUPIL, 32):
                 r = slice(r0, r0 + 32)
@@ -232,7 +266,7 @@
         for dc in range(1, NCASE):
             send(sig_buf.at[step, c], sig_buf.at[step, c], base, plane_device(0, 0, dc))
         if step == 0:
-            recon_copy.wait()
+            recon_load.wait()
         await_all(sig_buf.at[step, pl.ds(0, NCASE - 1)], base)
 
         signals = jnp.concatenate([sig_buf[step, k] for k in range(NCASE)], axis=0).astype(BF16)
@@ -277,13 +311,22 @@
 def body(turbulence, pupil_amp, mod_points, valid_pix, recon, gx, gy, act_map):
     rows, gt = sensor_tables()
     vmem = pl.BlockSpec(memory_space=pltpu.VMEM)
-    anywhere = pl.BlockSpec(memory_space=pl.ANY)
+    hbm = pl.BlockSpec(memory_space=pltpu.HBM)
     command, frame = pl.pallas_call(
         kernel,
         out_shape=(jax.ShapeDtypeStruct((40, 128), F32), jax.ShapeDtypeStruct((8, NF), F32)),
-        in_specs=[pl.BlockSpec(memory_space=pltpu.SMEM)] + [vmem] * 7 + [anywhere] * 2,
+        in_specs=[pl.BlockSpec(memory_space=pltpu.SMEM)] + [hbm] * 9,
         out_specs=(vmem, vmem),
         scratch_shapes=[
+            pltpu.VMEM((PUPIL, PUPIL), F32),
+            pltpu.VMEM((PUPIL, PUPIL), F32),
+            pltpu.VMEM((8, 128), jnp.int32),
+            pltpu.VMEM((40, 128), jnp.int32),
+            pltpu.VMEM((AY, PUPIL), F32),
+            pltpu.VMEM((AX, PUPIL), F32),
+            pltpu.VMEM((PUPIL, NF), BF16),
+            pltpu.VMEM((PUPIL, 3 * AY), BF16),
+            pltpu.VMEM((384, PUPIL), BF16),
             pltpu.VMEM((1280, 1024), BF16),
             pltpu.VMEM((2, 8, PUPIL), F32),
             pltpu.VMEM((8, 1, 128), F32),
@@ -305,15 +348,15 @@
             pltpu.VMEM((STEPS, NZ, 40, 128), BF16),
             pltpu.VMEM((40, 128), F32),
             pltpu.VMEM((64, 128), F32),
-            pltpu.SemaphoreType.DMA((2,)),
+            pltpu.SemaphoreType.DMA((9,)),
             pltpu.SemaphoreType.DMA((2 + 3 * STEPS,)),
             pltpu.SemaphoreType.DMA((2 + 3 * STEPS,)),
         ],
         compiler_params=pltpu.CompilerParams(
-            collective_id=0, has_side_effects=True, vmem_limit_bytes=40 * 1024 * 1024
+            collective_id=0, has_side_effects=True, vmem_limit_bytes=60 * 1024 * 1024
         ),
     )(
-        mod_points, turbulence[0], pupil_amp, valid_pix.reshape(8, 128), act_map.reshape(40, 128), gx, gy,
+        mod_points, turbulence[0], pupil_amp, valid_pix.reshape(8, 128), act_map.reshape(40, 128), gx.T, gy.T,
         jnp.asarray(gt).astype(BF16), jnp.asarray(rows), recon,
     )
     return command.reshape(1, 5120), frame[None]

time: 63.8 us -> 56.2 us (0.88)
  local copies, waits for them, and re-layouts: 10.3 us -> 2.66 us
    unnamed x18 -> x2, local copies, waits for them, and re-layouts: 10.3 us -> 2.66 us
where the time goes in v2:
time: 56.2 us; the launch traced here: 56 us
  Pallas kernels  52.1 us (93%)
  local copies, waits for them, and re-layouts  2.66 us (5%)
  between operations  1.29 us (2%)
    pallas_call x1, Pallas kernels, body(): pl.pallas_call(kernel, out_shape=(jax.ShapeDtypeStruct((40, 128), F32), j...  52.1 us
    unnamed x2, local copies, waits for them, and re-layouts  2.66 us

profile of v2, /device:TPU:4, one launch (start us, length us, event | category | flops | bytes accessed | tf_op | source)
XLA Modules:
  0.0 56.0 jit_solution(15195508799256059986)
XLA Ops:
  1.3 52.1 %shard_map.113 = (f32[40,128]{1,0:T(8,128)}, f32[8,512]{1,0:T(8,128)}) custom-call(s32[1]{0:T(128)S(6)} %copy.14.mod_ref, f32[256,256]{1,0:T(8,128)} %bitcast.7, f32[256,256]{1,0:T(8,128)} %amp_hbm.1, s32[8,128]{1,0:T(8,128)} %bitcast.13, s32[40,128]{1,0:T(8,128)} %bitcast.10, f32[64,256]{1,0:T(8,128)} %bitcast.9, f32[80,256]{1,0:T(8,128)} %bitcast.8, ...), custom_call_target="tpu_custom_call" | custom-call | tf_op jit(solution)/shard_map/pallas_call | solution.py:315
  53.4 1.3 %copy.15 = f32[1,5120]{1,0:T(1,128)} copy(f32[1,5120]{1,0:T(1,128)} %bitcast.11) | data formatting | bytes 40960
  54.7 1.3 %copy.16 = f32[1,8,512]{2,1,0:T(8,128)} copy(f32[1,8,512]{2,1,0:T(8,128)} %bitcast.12) | data formatting | bytes 32768

commit v3 on v2

--- a/solution.py
+++ b/solution.py
@@ -33,22 +33,21 @@
     turn = np.array([1, 1j, -1, -1j])[np.abs(k) % 4]
     m = (v * turn) @ w
     rows = np.stack([m.real, m.imag]).astype(np.float32)
-    return rows, m.imag.T.astype(np.float32)
+    return rows, 2.0 * m.imag.T.astype(np.float32)
 
 
 def sincos(x):
-    k = jnp.floor(x * (2.0 / math.pi) + 0.5)
-    r = ((x - k * 1.5703125) - k * 4.837512969970703e-4) - k * 7.549789948768648e-8
-    r2 = r * r
-    s = r + r * r2 * (-1.6666654611e-1 + r2 * (8.3321608736e-3 + r2 * -1.9515295891e-4))
-    c = 1.0 + r2 * (-0.5 + r2 * (4.166664568298827e-2 + r2 * (-1.388731625493765e-3 + r2 * 2.443315711809948e-5)))
-    q = k - 4.0 * jnp.floor(k * 0.25)
-    odd = (q == 1.0) | (q == 3.0)
-    sn = jnp.where(odd, c, s)
-    cs = jnp.where(odd, s, c)
-    sn = jnp.where(q >= 2.0, -sn, sn)
-    cs = jnp.where((q == 1.0) | (q == 2.0), -cs, cs)
-    return cs, sn
+    t = x * (0.5 / math.pi)
+    f = t - jnp.floor(t + 0.5)
+    g = f * f
+    s = 0.15457872399485673
+    for a in (-1.1961721628983193, 5.100079202734692, -10.33541503027875, 6.283185189118328):
+        s = s * g + a
+    s = s * f
+    c = -0.024431927347214694
+    for a in (0.23496099890009817, -1.3352176583726172, 4.058709736748474, -4.93480215997534, 1.0):
+        c = c * g + a
+    return 1.0 - 0.5 * (s * s), s * c
 
 
 def halves(x):
@@ -60,8 +59,8 @@
     mod_ref, turb_hbm, amp_hbm, pix_hbm, act_hbm, gx_hbm, gy_hbm, gt_hbm, rows_hbm, recon_hbm,
     cmd_out, frame_out,
     turb_ref, amp_ref, pix_ref, act_ref, gx_ref, gy_ref, gt_ref, gx_wide, gy_tall,
-    recon_ref, rows_ref, mod_a, mod_b, v_ref, l_ref, e_ref, x_ref, t_ref, y_ref,
-    oh_sig, oh_act, fr_ref, sig_buf, part_ref, part_bf, plane_buf, tot_ref, z_buf, gat_ref, grid_ref,
+    recon_ref, recon_t, rows_ref, mod_a, mod_b, v_ref, l_ref, e_ref, x_ref, t_ref, y_ref,
+    oh_sig, oh_act, fr_ref, sig_buf, part_bf, plane_buf, tot_ref, z_buf, gat_ref, grid_ref,
     local_sem, send_sem, recv_sem,
 ):
     c = lax.axis_index("case")
@@ -71,13 +70,20 @@
     yl = lax.rem(xy, NYL)
     x = lax.div(xy, NYL)
 
-    plane = [(dx, dy, dc) for dx in range(NX) for dy in range(NYL) for dc in range(NCASE) if (dx, dy, dc) != (0, 0, 0)]
-
-    def plane_device(dx, dy, dc):
+    high = lax.div(c, 2)
+    core = lax.rem(c, 2)
+
+    def hops(d):
+        return min(d[0], NX - d[0]) + (2 if d[2] and not d[1] else 1 if d[1] else 0)
+
+    plane = [(dx, fl, fh, fc) for dx in range(NX) for fl in range(2) for fh in range(2) for fc in range(2)]
+    plane = sorted(plane[1:], key=hops, reverse=True)
+    column = sorted(range(1, NZ), key=lambda d: min(d, NZ - d), reverse=True)
+
+    def plane_device(dx, fl, fh, fc):
         px = lax.rem(x + dx, NX)
-        py = lax.rem(yl + dy, NYL)
-        pc = lax.rem(c + dc, NCASE)
-        return pc, (px * NYL + py) * NZ + z
+        py = lax.rem(yl + fl, NYL)
+        return lax.rem(high + fh, 2) * 2 + lax.rem(core + fc, 2), (px * NYL + py) * NZ + z
 
     def z_device(dz):
         return c, xy * NZ + lax.rem(z + dz, NZ)
@@ -85,7 +91,7 @@
     barrier = pltpu.get_barrier_semaphore()
     for d in plane:
         pl.semaphore_signal(barrier, inc=1, device_id=plane_device(*d), device_id_type=MESH)
-    for dz in range(1, NZ):
+    for dz in column:
         pl.semaphore_signal(barrier, inc=1, device_id=z_device(dz), device_id_type=MESH)
 
     loads = [
@@ -137,6 +143,12 @@
         r = slice(r0, r0 + 32)
         make_field(r, turb_ref[r, :])
 
+    pl.semaphore_wait(barrier, len(plane) + NZ - 1)
+
+    near = [d for d in plane if d[2] == 0 and d[3] == 0]
+    for d in near:
+        send(mod_a.at[xy], mod_a.at[xy], 0, plane_device(*d))
+
     lane = lax.broadcasted_iota(jnp.int32, (128, 128), 0)
     pix_load.wait()
     local = pix_ref[...] - m * (8 * NF)
@@ -148,9 +160,11 @@
     act = act_ref[...]
     act_r = lax.rem(act, 128)
     act_q = lax.div(act, 128)
+    act_q = lax.rem(act_q, 5) * 8 + lax.div(act_q, 5)
     for s in range(40):
-        oh_act[:, 128 * s:128 * s + 128] = jnp.where(lane == act_r[s:s + 1, :], 1.0, 0.0).astype(BF16)
-    part_ref[...] = jnp.zeros_like(part_ref)
+        hot = jnp.where(lane == act_r[s:s + 1, :], 1.0, 0.0).astype(BF16)
+        oh_act[0:128, 128 * s:128 * s + 128] = hot
+        oh_act[128:256, 128 * s:128 * s + 128] = hot
     grid_ref[...] = jnp.zeros_like(grid_ref)
 
     gx_load.wait()
@@ -164,18 +178,16 @@
     gy_tall[0:AX, :] = gy_high
     gy_tall[128:128 + AX, :] = gy_high
     gy_tall[256:256 + AX, :] = gy_low
-    gt_load.wait()
-
-    pl.semaphore_wait(barrier, len(plane) + NZ - 1)
-
-    near = [(dx, dy) for dx in range(NX) for dy in range(NYL) if (dx, dy) != (0, 0)]
-    for dx, dy in near:
-        send(mod_a.at[xy], mod_a.at[xy], 0, plane_device(dx, dy, 0))
+
     await_all(mod_a.at[pl.ds(0, len(near))], 0)
     for j in range(NX * NYL):
         mod_b[z, j:j + 1, :] = mod_a[j]
-    for dz in range(1, NZ):
+    for dz in column:
         send(mod_b.at[z], mod_b.at[z], 1, z_device(dz))
+    recon_load.wait()
+    for i in range(10):
+        recon_t[:, 128 * i:128 * i + 128] = recon_ref[128 * i:128 * i + 128, :].T
+    gt_load.wait()
     await_all(mod_b.at[pl.ds(0, NZ - 1)], 1)
 
     angle = (2.0 * math.pi / POINTS) * mod_b[...].reshape(64, 128)
@@ -199,12 +211,12 @@
     for step in range(STEPS):
         if step > 0:
             total = tot_ref[step - 1]
-            high, low = halves(total)
-            picked = jnp.dot(jnp.concatenate([high, low], 0), oh_act[...], preferred_element_type=F32)
+            stacked = jnp.concatenate([total[:, 128 * t:128 * t + 128] for t in range(5)], axis=0)
+            picked = jnp.dot(jnp.concatenate(halves(stacked), axis=1), oh_act[...], preferred_element_type=F32)
             q_iota = lax.broadcasted_iota(jnp.int32, (40, 128), 0)
             for s in range(40):
                 cols = slice(128 * s, 128 * s + 128)
-                block = picked[0:40, cols] + picked[40:80, cols]
+                block = picked[:, cols]
                 gat_ref[s:s + 1, :] = jnp.sum(jnp.where(q_iota == act_q[s:s + 1, :], block, 0.0), axis=0, keepdims=True)
             for y8 in range(8):
                 s5, t = divmod(AX * y8, 128)
@@ -247,34 +259,31 @@
                 cols = slice(128 * q, 128 * q + 128)
                 src = 128 * (1 - q % 2)
                 r = slice(64 * i, 64 * i + 64)
-                dr = 0.5 * x_ref[r, src:src + 128] - y_ref[64 * i + 512:64 * i + 576, cols]
-                di = 0.5 * x_ref[r, src + PUPIL:src + PUPIL + 128] + y_ref[r, cols]
-                fr_ref[i:i + 1, cols] = jnp.sum(dr * dr + di * di, axis=0, keepdims=True) * (1.0 / 64)
+                dr = x_ref[r, src:src + 128] - y_ref[64 * i + 512:64 * i + 576, cols]
+                di = x_ref[r, src + PUPIL:src + PUPIL + 128] + y_ref[r, cols]
+                fr_ref[i:i + 1, cols] = jnp.sum(dr * dr + di * di, axis=0, keepdims=True) * (1.0 / 256)
         frame = fr_ref[...]
         if step == STEPS - 1:
             frame_out[...] = frame
 
-        stacked = jnp.concatenate([frame[:, 128 * q:128 * q + 128] for q in range(4)], axis=0).astype(BF16)
-        picked_sig = jnp.dot(stacked, oh_sig[...], preferred_element_type=F32)
+        tiles = jnp.concatenate([frame[:, 128 * q:128 * q + 128] for q in range(4)], axis=0).astype(BF16)
+        found = jnp.dot(tiles, oh_sig[...], preferred_element_type=F32)
         s_iota = lax.broadcasted_iota(jnp.int32, (32, 128), 0)
         for s in range(8):
             cols = slice(128 * s, 128 * s + 128)
             sig_buf[step, c, :, cols] = jnp.sum(
-                jnp.where(s_iota == pix_q[s:s + 1, :], picked_sig[:, cols], 0.0), axis=0, keepdims=True
+                jnp.where(s_iota == pix_q[s:s + 1, :], found[:, cols], 0.0), axis=0, keepdims=True
             )
         base = 2 + 3 * step
-        for dc in range(1, NCASE):
-            send(sig_buf.at[step, c], sig_buf.at[step, c], base, plane_device(0, 0, dc))
-        if step == 0:
-            recon_load.wait()
+        for fh, fc in ((1, 1), (1, 0), (0, 1)):
+            send(sig_buf.at[step, c], sig_buf.at[step, c], base, plane_device(0, 0, fh, fc))
         await_all(sig_buf.at[step, pl.ds(0, NCASE - 1)], base)
 
         signals = jnp.concatenate([sig_buf[step, k] for k in range(NCASE)], axis=0).astype(BF16)
-        part = lax.dot_general(signals, recon_ref[...], (((1,), (1,)), ((), ())), preferred_element_type=F32)
+        part = jnp.dot(signals, recon_t[...], preferred_element_type=F32)
         for k in range(NCASE):
-            for j in range(10):
-                part_ref[k, j:j + 1, :] = part[k:k + 1, 128 * j:128 * j + 128]
-        part_bf[step] = part_ref[...].astype(BF16)
+            rows = [part[k:k + 1, 640 * h:640 * h + 640] for h in range(2)]
+            part_bf[step, k] = jnp.concatenate(rows, axis=0).astype(BF16)
         plane_buf[step, xy * NCASE + c] = part_bf[step, c]
         for d in plane:
             device = plane_device(*d)
@@ -284,9 +293,9 @@
             acc = plane_buf[step, k].astype(F32)
             for j in range(1, NX * NYL):
                 acc = acc + plane_buf[step, j * NCASE + k].astype(F32)
-            tot_ref[step, 10 * k:10 * k + 10, :] = acc[0:10, :]
+            tot_ref[step, 2 * k:2 * k + 2, :] = acc
         z_buf[step, z] = tot_ref[step].astype(BF16)
-        for dz in range(1, NZ):
+        for dz in column:
             send(z_buf.at[step, z], z_buf.at[step, z], base + 2, z_device(dz))
         await_all(z_buf.at[step, pl.ds(0, NZ - 1)], base + 2)
         acc = z_buf[step, 0].astype(F32)
@@ -297,7 +306,8 @@
             acc = acc + tot_ref[step - 1]
         tot_ref[step] = acc
         if step == STEPS - 1:
-            cmd_out[...] = acc
+            for t in range(5):
+                cmd_out[pl.ds(t, 8, stride=5), :] = acc[:, 128 * t:128 * t + 128]
 
     await_sent(mod_a.at[pl.ds(0, len(near))], 0)
     await_sent(mod_b.at[pl.ds(0, NZ - 1)], 1)
@@ -314,7 +324,7 @@
     hbm = pl.BlockSpec(memory_space=pltpu.HBM)
     command, frame = pl.pallas_call(
         kernel,
-        out_shape=(jax.ShapeDtypeStruct((40, 128), F32), jax.ShapeDtypeStruct((8, NF), F32)),
+        out_shape=(pltpu.VMEM((40, 128), F32), pltpu.VMEM((8, NF), F32)),
         in_specs=[pl.BlockSpec(memory_space=pltpu.SMEM)] + [hbm] * 9,
         out_specs=(vmem, vmem),
         scratch_shapes=[
@@ -328,6 +338,7 @@
             pltpu.VMEM((PUPIL, 3 * AY), BF16),
             pltpu.VMEM((384, PUPIL), BF16),
             pltpu.VMEM((1280, 1024), BF16),
+            pltpu.VMEM((1024, 1280), BF16),
             pltpu.VMEM((2, 8, PUPIL), F32),
             pltpu.VMEM((8, 1, 128), F32),
             pltpu.VMEM((8, 8, 128), F32),
@@ -338,14 +349,13 @@
             pltpu.VMEM((1024, PUPIL), BF16),
             pltpu.VMEM((1024, NF), F32),
             pltpu.VMEM((128, 1024), BF16),
-            pltpu.VMEM((128, 5120), BF16),
+            pltpu.VMEM((256, 5120), BF16),
             pltpu.VMEM((8, NF), F32),
             pltpu.VMEM((STEPS, NCASE, 1, 1024), F32),
-            pltpu.VMEM((NCASE, 16, 128), F32),
-            pltpu.VMEM((STEPS, NCASE, 16, 128), BF16),
-            pltpu.VMEM((STEPS, 32, 16, 128), BF16),
-            pltpu.VMEM((STEPS, 40, 128), F32),
-            pltpu.VMEM((STEPS, NZ, 40, 128), BF16),
+            pltpu.VMEM((STEPS, NCASE, 2, 640), BF16),
+            pltpu.VMEM((STEPS, 32, 2, 640), BF16),
+            pltpu.VMEM((STEPS, 8, 640), F32),
+            pltpu.VMEM((STEPS, NZ, 8, 640), BF16),
             pltpu.VMEM((40, 128), F32),
             pltpu.VMEM((64, 128), F32),
             pltpu.SemaphoreType.DMA((9,)),

time: 56.2 us -> 50.8 us (0.904); the launches traced: 56 us -> 50 us
  Pallas kernels: 52.1 us -> 47.5 us
  local copies, waits for them, and re-layouts: 2.66 us -> 1.21 us
    pallas_call x1, Pallas kernels: 52.1 us -> 47.5 us  [body(): pl.pallas_call(kernel, out_shape=(pltpu.VMEM((40, 128), F32), pltpu.VMEM(...]
    unnamed x2, local copies, waits for them, and re-layouts: 2.66 us -> 1.21 us
where the time goes in v3:
time: 50.8 us; the launch traced here: 50 us
  Pallas kernels  47.5 us (94%)
  between operations  1.29 us (3%)
  local copies, waits for them, and re-layouts  1.21 us (2%)
    pallas_call x1, Pallas kernels, body(): pl.pallas_call(kernel, out_shape=(pltpu.VMEM((40, 128), F32), pltpu.VMEM(...  47.5 us
    unnamed x2, local copies, waits for them, and re-layouts  1.21 us

profile of v3, /device:TPU:4, one launch (start us, length us, event | category | flops | bytes accessed | tf_op | source)
XLA Modules:
  0.0 50.0 jit_solution(7489461573803968505)
XLA Ops:
  1.3 47.5 %shard_map.113 = (f32[40,128]{1,0:T(8,128)S(1)}, f32[8,512]{1,0:T(8,128)S(1)}) custom-call(s32[1]{0:T(128)S(6)} %copy.16.mod_ref, f32[256,256]{1,0:T(8,128)} %bitcast.9, f32[256,256]{1,0:T(8,128)} %amp_hbm.1, s32[8,128]{1,0:T(8,128)} %bitcast.13, s32[40,128]{1,0:T(8,128)} %bitcast.12, f32[64,256]{1,0:T(8,128)} %bitcast.11, f32[80,256]{1,0:T(8,128)} %bitcast.10, ...), custom_call_target="tpu_custom_call" | custom-call | tf_op jit(solution)/shard_map/pallas_call | solution.py:325
  48.8 0.6 %copy.14 = f32[1,5120]{1,0:T(1,128)} copy(f32[1,5120]{1,0:T(1,128)S(1)} %bitcast.7) | data formatting | bytes 40960
  49.4 0.6 %copy.15 = f32[1,8,512]{2,1,0:T(8,128)} copy(f32[1,8,512]{2,1,0:T(8,128)S(1)} %bitcast.8) | data formatting | bytes 32768

commit v4 on v3

--- a/solution.py
+++ b/solution.py
@@ -40,14 +40,14 @@
     t = x * (0.5 / math.pi)
     f = t - jnp.floor(t + 0.5)
     g = f * f
-    s = 0.15457872399485673
-    for a in (-1.1961721628983193, 5.100079202734692, -10.33541503027875, 6.283185189118328):
+    s = 0.10920575
+    for a in (-0.8457636, 3.60628896, -7.30824115, 4.44288283):
         s = s * g + a
     s = s * f
-    c = -0.024431927347214694
-    for a in (0.23496099890009817, -1.3352176583726172, 4.058709736748474, -4.93480215997534, 1.0):
+    c = 0.31124104
+    for a in (-1.88386521, 5.73951693, -6.97885475, 1.4142135623730951):
         c = c * g + a
-    return 1.0 - 0.5 * (s * s), s * c
+    return 1.0 - s * s, s * c
 
 
 def halves(x):
@@ -80,19 +80,17 @@
     plane = sorted(plane[1:], key=hops, reverse=True)
     column = sorted(range(1, NZ), key=lambda d: min(d, NZ - d), reverse=True)
 
+    at_x = [x * (NYL * NZ)] + [lax.rem(x + d, NX) * (NYL * NZ) for d in range(1, NX)]
+    at_yl = [yl * NZ, (1 - yl) * NZ]
+    at_z = [z] + [lax.rem(z + d, NZ) for d in range(1, NZ)]
+    at_high = [high * 2, (1 - high) * 2]
+    at_core = [core, 1 - core]
+
     def plane_device(dx, fl, fh, fc):
-        px = lax.rem(x + dx, NX)
-        py = lax.rem(yl + fl, NYL)
-        return lax.rem(high + fh, 2) * 2 + lax.rem(core + fc, 2), (px * NYL + py) * NZ + z
+        return at_high[fh] + at_core[fc], at_x[dx] + at_yl[fl] + z
 
     def z_device(dz):
-        return c, xy * NZ + lax.rem(z + dz, NZ)
-
-    barrier = pltpu.get_barrier_semaphore()
-    for d in plane:
-        pl.semaphore_signal(barrier, inc=1, device_id=plane_device(*d), device_id_type=MESH)
-    for dz in column:
-        pl.semaphore_signal(barrier, inc=1, device_id=z_device(dz), device_id_type=MESH)
+        return c, m - z + at_z[dz]
 
     loads = [
         pltpu.make_async_copy(src, dst, local_sem.at[i])
@@ -104,6 +102,12 @@
     ]
     for load in loads:
         load.start()
+    barrier = pltpu.get_barrier_semaphore()
+    for dz in column:
+        pl.semaphore_signal(barrier, inc=1, device_id=z_device(dz), device_id_type=MESH)
+    for d in plane:
+        pl.semaphore_signal(barrier, inc=1, device_id=plane_device(*d), device_id_type=MESH)
+
     turb_load, amp_load, pix_load, act_load, rows_load, gt_load, gx_load, gy_load, recon_load = loads
 
     def send(src, dst, phase, device):
@@ -162,9 +166,7 @@
     act_q = lax.div(act, 128)
     act_q = lax.rem(act_q, 5) * 8 + lax.div(act_q, 5)
     for s in range(40):
-        hot = jnp.where(lane == act_r[s:s + 1, :], 1.0, 0.0).astype(BF16)
-        oh_act[0:128, 128 * s:128 * s + 128] = hot
-        oh_act[128:256, 128 * s:128 * s + 128] = hot
+        oh_act[:, 128 * s:128 * s + 128] = jnp.where(lane == act_r[s:s + 1, :], 1.0, 0.0).astype(BF16)
     grid_ref[...] = jnp.zeros_like(grid_ref)
 
     gx_load.wait()
@@ -212,7 +214,7 @@
         if step > 0:
             total = tot_ref[step - 1]
             stacked = jnp.concatenate([total[:, 128 * t:128 * t + 128] for t in range(5)], axis=0)
-            picked = jnp.dot(jnp.concatenate(halves(stacked), axis=1), oh_act[...], preferred_element_type=F32)
+            picked = jnp.dot(stacked.astype(BF16), oh_act[...], preferred_element_type=F32)
             q_iota = lax.broadcasted_iota(jnp.int32, (40, 128), 0)
             for s in range(40):
                 cols = slice(128 * s, 128 * s + 128)
@@ -274,20 +276,24 @@
             sig_buf[step, c, :, cols] = jnp.sum(
                 jnp.where(s_iota == pix_q[s:s + 1, :], found[:, cols], 0.0), axis=0, keepdims=True
             )
-        base = 2 + 3 * step
-        for fh, fc in ((1, 1), (1, 0), (0, 1)):
-            send(sig_buf.at[step, c], sig_buf.at[step, c], base, plane_device(0, 0, fh, fc))
-        await_all(sig_buf.at[step, pl.ds(0, NCASE - 1)], base)
-
-        signals = jnp.concatenate([sig_buf[step, k] for k in range(NCASE)], axis=0).astype(BF16)
-        part = jnp.dot(signals, recon_t[...], preferred_element_type=F32)
-        for k in range(NCASE):
-            rows = [part[k:k + 1, 640 * h:640 * h + 640] for h in range(2)]
-            part_bf[step, k] = jnp.concatenate(rows, axis=0).astype(BF16)
-        plane_buf[step, xy * NCASE + c] = part_bf[step, c]
-        for d in plane:
-            device = plane_device(*d)
-            send(part_bf.at[step, device[0]], plane_buf.at[step, xy * NCASE + c], base + 1, device)
+        base = 2 + 4 * step
+        for fh, fc in ((1, 1), (1, 0)):
+            send(sig_buf.at[step, c], sig_buf.at[step, c], base + 3, plane_device(0, 0, fh, fc))
+        send(sig_buf.at[step, c], sig_buf.at[step, c], base, plane_device(0, 0, 0, 1))
+
+        for far in range(2):
+            await_all(sig_buf.at[step, pl.ds(0, 1 + far)], base + 3 * far)
+            pair = [sig_buf[step, at_high[far] + k] for k in range(2)]
+            part = jnp.dot(jnp.concatenate(pair, axis=0).astype(BF16), recon_t[...], preferred_element_type=F32)
+            for k in range(2):
+                rows = [part[k:k + 1, 640 * h:640 * h + 640] for h in range(2)]
+                part_bf[step, at_high[far] + k] = jnp.concatenate(rows, axis=0).astype(BF16)
+            if far == 0:
+                plane_buf[step, xy * NCASE + c] = part_bf[step, c]
+            for d in plane:
+                if d[2] == far:
+                    device = plane_device(*d)
+                    send(part_bf.at[step, device[0]], plane_buf.at[step, xy * NCASE + c], base + 1, device)
         await_all(plane_buf.at[step, pl.ds(0, len(plane))], base + 1)
         for k in range(NCASE):
             acc = plane_buf[step, k].astype(F32)
@@ -312,8 +318,9 @@
     await_sent(mod_a.at[pl.ds(0, len(near))], 0)
     await_sent(mod_b.at[pl.ds(0, NZ - 1)], 1)
     for step in range(STEPS):
-        base = 2 + 3 * step
-        await_sent(sig_buf.at[step, pl.ds(0, NCASE - 1)], base)
+        base = 2 + 4 * step
+        await_sent(sig_buf.at[step, pl.ds(0, 1)], base)
+        await_sent(sig_buf.at[step, pl.ds(0, 2)], base + 3)
         await_sent(plane_buf.at[step, pl.ds(0, len(plane))], base + 1)
         await_sent(z_buf.at[step, pl.ds(0, NZ - 1)], base + 2)
 
@@ -349,7 +356,7 @@
             pltpu.VMEM((1024, PUPIL), BF16),
             pltpu.VMEM((1024, NF), F32),
             pltpu.VMEM((128, 1024), BF16),
-            pltpu.VMEM((256, 5120), BF16),
+            pltpu.VMEM((128, 5120), BF16),
             pltpu.VMEM((8, NF), F32),
             pltpu.VMEM((STEPS, NCASE, 1, 1024), F32),
             pltpu.VMEM((STEPS, NCASE, 2, 640), BF16),
@@ -359,8 +366,8 @@
             pltpu.VMEM((40, 128), F32),
             pltpu.VMEM((64, 128), F32),
             pltpu.SemaphoreType.DMA((9,)),
-            pltpu.SemaphoreType.DMA((2 + 3 * STEPS,)),
-            pltpu.SemaphoreType.DMA((2 + 3 * STEPS,)),
+            pltpu.SemaphoreType.DMA((2 + 4 * STEPS,)),
+            pltpu.SemaphoreType.DMA((2 + 4 * STEPS,)),
         ],
         compiler_params=pltpu.CompilerParams(
             collective_id=0, has_side_effects=True, vmem_limit_bytes=60 * 1024 * 1024

time: 50.8 us -> 51.1 us (level)
  no operation moved by 1% of the time
where the time goes in v4:
time: 51.1 us; the launch traced here: 50.1 us
  Pallas kernels  47.6 us (93%)
  between operations  1.29 us (3%)
  local copies, waits for them, and re-layouts  1.21 us (2%)
    pallas_call x1, Pallas kernels, body(): pl.pallas_call(kernel, out_shape=(pltpu.VMEM((40, 128), F32), pltpu.VMEM(...  47.6 us
    unnamed x2, local copies, waits for them, and re-layouts  1.21 us

profile of v4, /device:TPU:4, one launch (start us, length us, event | category | flops | bytes accessed | tf_op | source)
XLA Modules:
  0.0 50.1 jit_solution(12600368925820309414)
XLA Ops:
  1.3 47.6 %shard_map.113 = (f32[40,128]{1,0:T(8,128)S(1)}, f32[8,512]{1,0:T(8,128)S(1)}) custom-call(s32[1]{0:T(128)S(6)} %copy.16.mod_ref, f32[256,256]{1,0:T(8,128)} %bitcast.9, f32[256,256]{1,0:T(8,128)} %amp_hbm.1, s32[8,128]{1,0:T(8,128)} %bitcast.13, s32[40,128]{1,0:T(8,128)} %bitcast.12, f32[64,256]{1,0:T(8,128)} %bitcast.11, f32[80,256]{1,0:T(8,128)} %bitcast.10, ...), custom_call_target="tpu_custom_call" | custom-call | tf_op jit(solution)/shard_map/pallas_call | solution.py:332
  48.9 0.6 %copy.14 = f32[1,5120]{1,0:T(1,128)} copy(f32[1,5120]{1,0:T(1,128)S(1)} %bitcast.7) | data formatting | bytes 40960
  49.5 0.6 %copy.15 = f32[1,8,512]{2,1,0:T(8,128)} copy(f32[1,8,512]{2,1,0:T(8,128)S(1)} %bitcast.8) | data formatting | bytes 32768

commit v5 on v4

--- a/solution.py
+++ b/solution.py
@@ -20,6 +20,7 @@
 NX, NYL, NZ = 4, 2, 8
 NCASE = 4
 MESH = pl.DeviceIdType.MESH
+FIELD = 2 + 3 * STEPS
 F32 = jnp.float32
 BF16 = jnp.bfloat16
 
@@ -59,7 +60,7 @@
     mod_ref, turb_hbm, amp_hbm, pix_hbm, act_hbm, gx_hbm, gy_hbm, gt_hbm, rows_hbm, recon_hbm,
     cmd_out, frame_out,
     turb_ref, amp_ref, pix_ref, act_ref, gx_ref, gy_ref, gt_ref, gx_wide, gy_tall,
-    recon_ref, recon_t, rows_ref, mod_a, mod_b, v_ref, l_ref, e_ref, x_ref, t_ref, y_ref,
+    recon_ref, recon_t, rows_ref, mod_a, mod_b, v_ref, l_ref, e_ref, e_other, x_ref, t_ref, y_ref,
     oh_sig, oh_act, fr_ref, sig_buf, part_bf, plane_buf, tot_ref, z_buf, gat_ref, grid_ref,
     local_sem, send_sem, recv_sem,
 ):
@@ -152,6 +153,7 @@
     near = [d for d in plane if d[2] == 0 and d[3] == 0]
     for d in near:
         send(mod_a.at[xy], mod_a.at[xy], 0, plane_device(*d))
+    send(e_ref.at[pl.ds(0, PUPIL)], e_other.at[pl.ds(0, PUPIL)], FIELD, plane_device(0, 1, 1, 0))
 
     lane = lax.broadcasted_iota(jnp.int32, (128, 128), 0)
     pix_load.wait()
@@ -210,9 +212,46 @@
             l_ref[64 * i:64 * i + 64, cols] = (mr * ur - mi * ui).astype(BF16)
             l_ref[64 * i:64 * i + 64, 128 * h + PUPIL:128 * h + PUPIL + 128] = (mr * ui + mi * ur).astype(BF16)
 
+    def compute_frame(field):
+        x_ref[...] = jnp.dot(l_ref[...], field[...], preferred_element_type=F32)
+        for i in range(8):
+            r = slice(64 * i, 64 * i + 64)
+            xr = x_ref[r, 0:PUPIL]
+            xi = x_ref[r, PUPIL:]
+            vr = v_ref[0]
+            vi = v_ref[1]
+            tr = xr * vr - xi * vi
+            ti = xr * vi + xi * vr
+            x_ref[r, 0:PUPIL] = tr
+            x_ref[r, PUPIL:] = ti
+            t_ref[r, :] = tr.astype(BF16)
+            t_ref[64 * i + 512:64 * i + 576, :] = ti.astype(BF16)
+        y_ref[...] = jnp.dot(t_ref[...], gt_ref[...], preferred_element_type=F32)
+        for i in range(8):
+            for q in range(4):
+                cols = slice(128 * q, 128 * q + 128)
+                src = 128 * (1 - q % 2)
+                r = slice(64 * i, 64 * i + 64)
+                dr = x_ref[r, src:src + 128] - y_ref[64 * i + 512:64 * i + 576, cols]
+                di = x_ref[r, src + PUPIL:src + PUPIL + 128] + y_ref[r, cols]
+                fr_ref[i:i + 1, cols] = jnp.sum(dr * dr + di * di, axis=0, keepdims=True) * (1.0 / 256)
+        return fr_ref[...]
+
+    def select_signals(frame, slot):
+        tiles = jnp.concatenate([frame[:, 128 * q:128 * q + 128] for q in range(4)], axis=0).astype(BF16)
+        found = jnp.dot(tiles, oh_sig[...], preferred_element_type=F32)
+        s_iota = lax.broadcasted_iota(jnp.int32, (32, 128), 0)
+        for s in range(8):
+            cols = slice(128 * s, 128 * s + 128)
+            slot[:, cols] = jnp.sum(
+                jnp.where(s_iota == pix_q[s:s + 1, :], found[:, cols], 0.0), axis=0, keepdims=True
+            )
+
     for step in range(STEPS):
         if step > 0:
             total = tot_ref[step - 1]
+            if step == 1:
+                await_sent(e_ref.at[pl.ds(0, PUPIL)], FIELD)
             stacked = jnp.concatenate([total[:, 128 * t:128 * t + 128] for t in range(5)], axis=0)
             picked = jnp.dot(stacked.astype(BF16), oh_act[...], preferred_element_type=F32)
             q_iota = lax.broadcasted_iota(jnp.int32, (40, 128), 0)
@@ -242,58 +281,34 @@
                 r = slice(r0, r0 + 32)
                 make_field(r, turb_ref[r, :] - surface[r, :])
 
-        x_ref[...] = jnp.dot(l_ref[...], e_ref[...], preferred_element_type=F32)
-        for i in range(8):
-            r = slice(64 * i, 64 * i + 64)
-            xr = x_ref[r, 0:PUPIL]
-            xi = x_ref[r, PUPIL:]
-            vr = v_ref[0]
-            vi = v_ref[1]
-            tr = xr * vr - xi * vi
-            ti = xr * vi + xi * vr
-            x_ref[r, 0:PUPIL] = tr
-            x_ref[r, PUPIL:] = ti
-            t_ref[r, :] = tr.astype(BF16)
-            t_ref[64 * i + 512:64 * i + 576, :] = ti.astype(BF16)
-        y_ref[...] = jnp.dot(t_ref[...], gt_ref[...], preferred_element_type=F32)
-        for i in range(8):
-            for q in range(4):
-                cols = slice(128 * q, 128 * q + 128)
-                src = 128 * (1 - q % 2)
-                r = slice(64 * i, 64 * i + 64)
-                dr = x_ref[r, src:src + 128] - y_ref[64 * i + 512:64 * i + 576, cols]
-                di = x_ref[r, src + PUPIL:src + PUPIL + 128] + y_ref[r, cols]
-                fr_ref[i:i + 1, cols] = jnp.sum(dr * dr + di * di, axis=0, keepdims=True) * (1.0 / 256)
-        frame = fr_ref[...]
+        frame = compute_frame(e_ref)
         if step == STEPS - 1:
             frame_out[...] = frame
 
-        tiles = jnp.concatenate([frame[:, 128 * q:128 * q + 128] for q in range(4)], axis=0).astype(BF16)
-        found = jnp.dot(tiles, oh_sig[...], preferred_element_type=F32)
-        s_iota = lax.broadcasted_iota(jnp.int32, (32, 128), 0)
-        for s in range(8):
-            cols = slice(128 * s, 128 * s + 128)
-            sig_buf[step, c, :, cols] = jnp.sum(
-                jnp.where(s_iota == pix_q[s:s + 1, :], found[:, cols], 0.0), axis=0, keepdims=True
-            )
-        base = 2 + 4 * step
-        for fh, fc in ((1, 1), (1, 0)):
-            send(sig_buf.at[step, c], sig_buf.at[step, c], base + 3, plane_device(0, 0, fh, fc))
-        send(sig_buf.at[step, c], sig_buf.at[step, c], base, plane_device(0, 0, 0, 1))
-
-        for far in range(2):
-            await_all(sig_buf.at[step, pl.ds(0, 1 + far)], base + 3 * far)
-            pair = [sig_buf[step, at_high[far] + k] for k in range(2)]
-            part = jnp.dot(jnp.concatenate(pair, axis=0).astype(BF16), recon_t[...], preferred_element_type=F32)
-            for k in range(2):
-                rows = [part[k:k + 1, 640 * h:640 * h + 640] for h in range(2)]
-                part_bf[step, at_high[far] + k] = jnp.concatenate(rows, axis=0).astype(BF16)
-            if far == 0:
-                plane_buf[step, xy * NCASE + c] = part_bf[step, c]
-            for d in plane:
-                if d[2] == far:
-                    device = plane_device(*d)
-                    send(part_bf.at[step, device[0]], plane_buf.at[step, xy * NCASE + c], base + 1, device)
+        select_signals(frame, sig_buf.at[step, c])
+        base = 2 + 3 * step
+        if step == 0:
+            other = at_high[1] + core
+            send(sig_buf.at[step, c], sig_buf.at[step, c], base, plane_device(0, 0, 0, 1))
+            await_all(e_other.at[pl.ds(0, PUPIL)], FIELD)
+            e_other[PUPIL:, 0:PUPIL] = -e_other[0:PUPIL, PUPIL:]
+            e_other[PUPIL:, PUPIL:] = e_other[0:PUPIL, 0:PUPIL]
+            select_signals(compute_frame(e_other), sig_buf.at[step, other])
+            send(sig_buf.at[step, other], sig_buf.at[step, other], base, plane_device(0, 0, 0, 1))
+            await_all(sig_buf.at[step, pl.ds(0, 2)], base)
+        else:
+            for fh, fc in ((1, 1), (1, 0), (0, 1)):
+                send(sig_buf.at[step, c], sig_buf.at[step, c], base, plane_device(0, 0, fh, fc))
+            await_all(sig_buf.at[step, pl.ds(0, 3)], base)
+        signals = jnp.concatenate([sig_buf[step, k] for k in range(NCASE)], axis=0).astype(BF16)
+        part = jnp.dot(signals, recon_t[...], preferred_element_type=F32)
+        for k in range(NCASE):
+            rows = [part[k:k + 1, 640 * h:640 * h + 640] for h in range(2)]
+            part_bf[step, k] = jnp.concatenate(rows, axis=0).astype(BF16)
+        plane_buf[step, xy * NCASE + c] = part_bf[step, c]
+        for d in plane:
+            device = plane_device(*d)
+            send(part_bf.at[step, device[0]], plane_buf.at[step, xy * NCASE + c], base + 1, device)
         await_all(plane_buf.at[step, pl.ds(0, len(plane))], base + 1)
         for k in range(NCASE):
             acc = plane_buf[step, k].astype(F32)
@@ -318,9 +333,8 @@
     await_sent(mod_a.at[pl.ds(0, len(near))], 0)
     await_sent(mod_b.at[pl.ds(0, NZ - 1)], 1)
     for step in range(STEPS):
-        base = 2 + 4 * step
-        await_sent(sig_buf.at[step, pl.ds(0, 1)], base)
-        await_sent(sig_buf.at[step, pl.ds(0, 2)], base + 3)
+        base = 2 + 3 * step
+        await_sent(sig_buf.at[step, pl.ds(0, 2 + step)], base)
         await_sent(plane_buf.at[step, pl.ds(0, len(plane))], base + 1)
         await_sent(z_buf.at[step, pl.ds(0, NZ - 1)], base + 2)
 
@@ -352,6 +366,7 @@
             pltpu.VMEM((2, 64, PUPIL), F32),
             pltpu.VMEM((512, 512), BF16),
             pltpu.VMEM((512, 512), BF16),
+            pltpu.VMEM((512, 512), BF16),
             pltpu.VMEM((512, 512), F32),
             pltpu.VMEM((1024, PUPIL), BF16),
             pltpu.VMEM((1024, NF), F32),
@@ -366,8 +381,8 @@
             pltpu.VMEM((40, 128), F32),
             pltpu.VMEM((64, 128), F32),
             pltpu.SemaphoreType.DMA((9,)),
-            pltpu.SemaphoreType.DMA((2 + 4 * STEPS,)),
-            pltpu.SemaphoreType.DMA((2 + 4 * STEPS,)),
+            pltpu.SemaphoreType.DMA((3 + 3 * STEPS,)),
+            pltpu.SemaphoreType.DMA((3 + 3 * STEPS,)),
         ],
         compiler_params=pltpu.CompilerParams(
             collective_id=0, has_side_effects=True, vmem_limit_bytes=60 * 1024 * 1024

time: 51.1 us -> 48.8 us (0.955)
  the two profiles are of different devices: /device:TPU:4 before, /device:TPU:1 now
where the time goes in v5:
time: 48.8 us; the launch traced here: 48.7 us
  Pallas kernels  46.2 us (95%)
  between operations  1.29 us (3%)
  local copies, waits for them, and re-layouts  1.21 us (2%)
    pallas_call x1, Pallas kernels, body(): pl.pallas_call(kernel, out_shape=(pltpu.VMEM((40, 128), F32), pltpu.VMEM(...  46.2 us
    unnamed x2, local copies, waits for them, and re-layouts  1.21 us

profile of v5, /device:TPU:1, one launch (start us, length us, event | category | flops | bytes accessed | tf_op | source)
XLA Modules:
  0.0 48.7 jit_solution(14728333006826021384)
XLA Ops:
  1.3 46.2 %shard_map.113 = (f32[40,128]{1,0:T(8,128)S(1)}, f32[8,512]{1,0:T(8,128)S(1)}) custom-call(s32[1]{0:T(128)S(6)} %copy.16.mod_ref, f32[256,256]{1,0:T(8,128)} %bitcast.9, f32[256,256]{1,0:T(8,128)} %amp_hbm.1, s32[8,128]{1,0:T(8,128)} %bitcast.13, s32[40,128]{1,0:T(8,128)} %bitcast.12, f32[64,256]{1,0:T(8,128)} %bitcast.11, f32[80,256]{1,0:T(8,128)} %bitcast.10, ...), custom_call_target="tpu_custom_call" | custom-call | tf_op jit(solution)/shard_map/pallas_call | solution.py:346
  47.5 0.6 %copy.14 = f32[1,5120]{1,0:T(1,128)} copy(f32[1,5120]{1,0:T(1,128)S(1)} %bitcast.7) | data formatting | bytes 40960
  48.1 0.6 %copy.15 = f32[1,8,512]{2,1,0:T(8,128)} copy(f32[1,8,512]{2,1,0:T(8,128)S(1)} %bitcast.8) | data formatting | bytes 32768

commit v6 on v5

--- a/solution.py
+++ b/solution.py
@@ -20,7 +20,7 @@
 NX, NYL, NZ = 4, 2, 8
 NCASE = 4
 MESH = pl.DeviceIdType.MESH
-FIELD = 2 + 3 * STEPS
+FIELD, PIXELS, FRAME = 2 + 3 * STEPS, 3 + 3 * STEPS, 4 + 3 * STEPS
 F32 = jnp.float32
 BF16 = jnp.bfloat16
 
@@ -60,7 +60,7 @@
     mod_ref, turb_hbm, amp_hbm, pix_hbm, act_hbm, gx_hbm, gy_hbm, gt_hbm, rows_hbm, recon_hbm,
     cmd_out, frame_out,
     turb_ref, amp_ref, pix_ref, act_ref, gx_ref, gy_ref, gt_ref, gx_wide, gy_tall,
-    recon_ref, recon_t, rows_ref, mod_a, mod_b, v_ref, l_ref, e_ref, e_other, x_ref, t_ref, y_ref,
+    recon_ref, recon_t, rows_ref, near_rows_ref, near_pix, frame_in, sig_out, u_ref, mod_a, mod_b, v_ref, l_ref, e_ref, e_other, x_ref, t_ref, y_ref,
     oh_sig, oh_act, fr_ref, sig_buf, part_bf, plane_buf, tot_ref, z_buf, gat_ref, grid_ref,
     local_sem, send_sem, recv_sem,
 ):
@@ -71,6 +71,7 @@
     yl = lax.rem(xy, NYL)
     x = lax.div(xy, NYL)
 
+    near_m = m + (1 - 2 * yl) * NZ
     high = lax.div(c, 2)
     core = lax.rem(c, 2)
 
@@ -99,6 +100,7 @@
             (turb_hbm, turb_ref), (amp_hbm, amp_ref), (pix_hbm, pix_ref), (act_hbm, act_ref),
             (rows_hbm.at[:, pl.ds(pl.multiple_of(m * 8, 8), 8), :], rows_ref), (gt_hbm, gt_ref),
             (gx_hbm, gx_ref), (gy_hbm, gy_ref), (recon_hbm, recon_ref),
+            (rows_hbm.at[:, pl.ds(pl.multiple_of(near_m * 8, 8), 8), :], near_rows_ref),
         ))
     ]
     for load in loads:
@@ -109,7 +111,7 @@
     for d in plane:
         pl.semaphore_signal(barrier, inc=1, device_id=plane_device(*d), device_id_type=MESH)
 
-    turb_load, amp_load, pix_load, act_load, rows_load, gt_load, gx_load, gy_load, recon_load = loads
+    turb_load, amp_load, pix_load, act_load, rows_load, gt_load, gx_load, gy_load, recon_load, near_rows_load = loads
 
     def send(src, dst, phase, device):
         pltpu.make_async_remote_copy(
@@ -157,11 +159,16 @@
 
     lane = lax.broadcasted_iota(jnp.int32, (128, 128), 0)
     pix_load.wait()
-    local = pix_ref[...] - m * (8 * NF)
-    pix_r = lax.rem(local, 128)
-    pix_q = lax.rem(lax.div(local, 128), 4) * 8 + lax.div(local, NF)
-    for s in range(8):
-        oh_sig[:, 128 * s:128 * s + 128] = jnp.where(lane == pix_r[s:s + 1, :], 1.0, 0.0).astype(BF16)
+    send(pix_ref, near_pix, PIXELS, plane_device(0, 1, 0, 0))
+
+    def pixel_table(pixels, block):
+        local = pixels - block * (8 * NF)
+        pix_r = lax.rem(local, 128)
+        for s in range(8):
+            oh_sig[:, 128 * s:128 * s + 128] = jnp.where(lane == pix_r[s:s + 1, :], 1.0, 0.0).astype(BF16)
+        return lax.rem(lax.div(local, 128), 4) * 8 + lax.div(local, NF)
+
+    pix_q = pixel_table(pix_ref[...], m)
     act_load.wait()
     act = act_ref[...]
     act_r = lax.rem(act, 128)
@@ -198,7 +205,6 @@
     ca, sa = sincos(angle)
     centred = lax.broadcasted_iota(jnp.int32, (64, 128), 1).astype(F32)
     scale = 2.0 * math.pi * RADIUS / NF
-    rows_load.wait()
     for h in range(2):
         pos = scale * (centred + (128.0 * h - PUPIL // 2))
         cols = slice(128 * h, 128 * h + 128)
@@ -206,11 +212,23 @@
         v_ref[0, :, cols] = vr
         v_ref[1, :, cols] = vi
         ur, ui = sincos(pos * ca)
-        for i in range(8):
-            mr = rows_ref[0, i:i + 1, cols]
-            mi = rows_ref[1, i:i + 1, cols]
-            l_ref[64 * i:64 * i + 64, cols] = (mr * ur - mi * ui).astype(BF16)
-            l_ref[64 * i:64 * i + 64, 128 * h + PUPIL:128 * h + PUPIL + 128] = (mr * ui + mi * ur).astype(BF16)
+        u_ref[0, :, cols] = ur
+        u_ref[1, :, cols] = ui
+
+    def left_factor(table):
+        for h in range(2):
+            cols = slice(128 * h, 128 * h + 128)
+            ur = u_ref[0, :, cols]
+            ui = u_ref[1, :, cols]
+            for i in range(8):
+                mr = table[0, i:i + 1, cols]
+                mi = table[1, i:i + 1, cols]
+                r = slice(64 * i, 64 * i + 64)
+                l_ref[r, cols] = (mr * ur - mi * ui).astype(BF16)
+                l_ref[r, 128 * h + PUPIL:128 * h + PUPIL + 128] = (mr * ui + mi * ur).astype(BF16)
+
+    rows_load.wait()
+    left_factor(rows_ref)
 
     def compute_frame(field):
         x_ref[...] = jnp.dot(l_ref[...], field[...], preferred_element_type=F32)
@@ -237,7 +255,7 @@
                 fr_ref[i:i + 1, cols] = jnp.sum(dr * dr + di * di, axis=0, keepdims=True) * (1.0 / 256)
         return fr_ref[...]
 
-    def select_signals(frame, slot):
+    def select_signals(frame, pix_q, slot):
         tiles = jnp.concatenate([frame[:, 128 * q:128 * q + 128] for q in range(4)], axis=0).astype(BF16)
         found = jnp.dot(tiles, oh_sig[...], preferred_element_type=F32)
         s_iota = lax.broadcasted_iota(jnp.int32, (32, 128), 0)
@@ -282,24 +300,23 @@
                 make_field(r, turb_ref[r, :] - surface[r, :])
 
         frame = compute_frame(e_ref)
-        if step == STEPS - 1:
-            frame_out[...] = frame
-
-        select_signals(frame, sig_buf.at[step, c])
         base = 2 + 3 * step
         if step == 0:
+            select_signals(frame, pix_q, sig_buf.at[step, c])
             other = at_high[1] + core
             send(sig_buf.at[step, c], sig_buf.at[step, c], base, plane_device(0, 0, 0, 1))
             await_all(e_other.at[pl.ds(0, PUPIL)], FIELD)
             e_other[PUPIL:, 0:PUPIL] = -e_other[0:PUPIL, PUPIL:]
             e_other[PUPIL:, PUPIL:] = e_other[0:PUPIL, 0:PUPIL]
-            select_signals(compute_frame(e_other), sig_buf.at[step, other])
+            select_signals(compute_frame(e_other), pix_q, sig_buf.at[step, other])
             send(sig_buf.at[step, other], sig_buf.at[step, other], base, plane_device(0, 0, 0, 1))
             await_all(sig_buf.at[step, pl.ds(0, 2)], base)
         else:
-            for fh, fc in ((1, 1), (1, 0), (0, 1)):
-                send(sig_buf.at[step, c], sig_buf.at[step, c], base, plane_device(0, 0, fh, fc))
-            await_all(sig_buf.at[step, pl.ds(0, 3)], base)
+            select_signals(frame, pix_q, sig_out)
+            for fh, fc in ((1, 1), (0, 1), (1, 0), (0, 0)):
+                send(sig_out, sig_buf.at[step, c], base, plane_device(0, 1, fh, fc))
+            send(fr_ref, frame_in, FRAME, plane_device(0, 1, 0, 0))
+            await_all(sig_buf.at[step], base)
         signals = jnp.concatenate([sig_buf[step, k] for k in range(NCASE)], axis=0).astype(BF16)
         part = jnp.dot(signals, recon_t[...], preferred_element_type=F32)
         for k in range(NCASE):
@@ -309,6 +326,11 @@
         for d in plane:
             device = plane_device(*d)
             send(part_bf.at[step, device[0]], plane_buf.at[step, xy * NCASE + c], base + 1, device)
+        if step == 0:
+            await_all(near_pix, PIXELS)
+            pix_q = pixel_table(near_pix[...], near_m)
+            near_rows_load.wait()
+            left_factor(near_rows_ref)
         await_all(plane_buf.at[step, pl.ds(0, len(plane))], base + 1)
         for k in range(NCASE):
             acc = plane_buf[step, k].astype(F32)
@@ -327,14 +349,18 @@
             acc = acc + tot_ref[step - 1]
         tot_ref[step] = acc
         if step == STEPS - 1:
+            await_all(frame_in, FRAME)
+            frame_out[...] = frame_in[...]
             for t in range(5):
                 cmd_out[pl.ds(t, 8, stride=5), :] = acc[:, 128 * t:128 * t + 128]
 
+    await_sent(pix_ref, PIXELS)
+    await_sent(fr_ref, FRAME)
     await_sent(mod_a.at[pl.ds(0, len(near))], 0)
     await_sent(mod_b.at[pl.ds(0, NZ - 1)], 1)
     for step in range(STEPS):
         base = 2 + 3 * step
-        await_sent(sig_buf.at[step, pl.ds(0, 2 + step)], base)
+        await_sent(sig_buf.at[step, pl.ds(0, 2 + 2 * step)], base)
         await_sent(plane_buf.at[step, pl.ds(0, len(plane))], base + 1)
         await_sent(z_buf.at[step, pl.ds(0, NZ - 1)], base + 2)
 
@@ -361,6 +387,11 @@
             pltpu.VMEM((1280, 1024), BF16),
             pltpu.VMEM((1024, 1280), BF16),
             pltpu.VMEM((2, 8, PUPIL), F32),
+            pltpu.VMEM((2, 8, PUPIL), F32),
+            pltpu.VMEM((8, 128), jnp.int32),
+            pltpu.VMEM((8, NF), F32),
+            pltpu.VMEM((1, 1024), F32),
+            pltpu.VMEM((2, 64, PUPIL), F32),
             pltpu.VMEM((8, 1, 128), F32),
             pltpu.VMEM((8, 8, 128), F32),
             pltpu.VMEM((2, 64, PUPIL), F32),
@@ -380,9 +411,9 @@
             pltpu.VMEM((STEPS, NZ, 8, 640), BF16),
             pltpu.VMEM((40, 128), F32),
             pltpu.VMEM((64, 128), F32),
-            pltpu.SemaphoreType.DMA((9,)),
-            pltpu.SemaphoreType.DMA((3 + 3 * STEPS,)),
-            pltpu.SemaphoreType.DMA((3 + 3 * STEPS,)),
+            pltpu.SemaphoreType.DMA((10,)),
+            pltpu.SemaphoreType.DMA((5 + 3 * STEPS,)),
+            pltpu.SemaphoreType.DMA((5 + 3 * STEPS,)),
         ],
         compiler_params=pltpu.CompilerParams(
             collective_id=0, has_side_effects=True, vmem_limit_bytes=60 * 1024 * 1024

time: 48.8 us -> 48.8 us (level)
  no operation moved by 1% of the time
where the time goes in v6:
time: 48.8 us; the launch traced here: 48.7 us
  Pallas kernels  46.2 us (95%)
  between operations  1.29 us (3%)
  local copies, waits for them, and re-layouts  1.21 us (2%)
    pallas_call x1, Pallas kernels, body(): pl.pallas_call(kernel, out_shape=(pltpu.VMEM((40, 128), F32), pltpu.VMEM(...  46.2 us
    unnamed x2, local copies, waits for them, and re-layouts  1.21 us

profile of v6, /device:TPU:1, one launch (start us, length us, event | category | flops | bytes accessed | tf_op | source)
XLA Modules:
  0.0 48.7 jit_solution(4467329263161460727)
XLA Ops:
  1.3 46.2 %shard_map.113 = (f32[40,128]{1,0:T(8,128)S(1)}, f32[8,512]{1,0:T(8,128)S(1)}) custom-call(s32[1]{0:T(128)S(6)} %copy.16.mod_ref, f32[256,256]{1,0:T(8,128)} %bitcast.9, f32[256,256]{1,0:T(8,128)} %amp_hbm.1, s32[8,128]{1,0:T(8,128)} %bitcast.13, s32[40,128]{1,0:T(8,128)} %bitcast.12, f32[64,256]{1,0:T(8,128)} %bitcast.11, f32[80,256]{1,0:T(8,128)} %bitcast.10, ...), custom_call_target="tpu_custom_call" | custom-call | tf_op jit(solution)/shard_map/pallas_call | solution.py:372
  47.5 0.6 %copy.14 = f32[1,5120]{1,0:T(1,128)} copy(f32[1,5120]{1,0:T(1,128)S(1)} %bitcast.7) | data formatting | bytes 40960
  48.1 0.6 %copy.15 = f32[1,8,512]{2,1,0:T(8,128)} copy(f32[1,8,512]{2,1,0:T(8,128)S(1)} %bitcast.8) | data formatting | bytes 32768

commit v7 on v5

--- a/solution.py
+++ b/solution.py
@@ -20,7 +20,7 @@
 NX, NYL, NZ = 4, 2, 8
 NCASE = 4
 MESH = pl.DeviceIdType.MESH
-FIELD = 2 + 3 * STEPS
+FIELD, RECON = 2 + 3 * STEPS, 3 + 3 * STEPS
 F32 = jnp.float32
 BF16 = jnp.bfloat16
 
@@ -77,18 +77,20 @@
     def hops(d):
         return min(d[0], NX - d[0]) + (2 if d[2] and not d[1] else 1 if d[1] else 0)
 
-    plane = [(dx, fl, fh, fc) for dx in range(NX) for fl in range(2) for fh in range(2) for fc in range(2)]
+    plane = [(dx, fl, fh) for dx in range(NX) for fl in range(2) for fh in range(2)]
     plane = sorted(plane[1:], key=hops, reverse=True)
     column = sorted(range(1, NZ), key=lambda d: min(d, NZ - d), reverse=True)
 
     at_x = [x * (NYL * NZ)] + [lax.rem(x + d, NX) * (NYL * NZ) for d in range(1, NX)]
     at_yl = [yl * NZ, (1 - yl) * NZ]
     at_z = [z] + [lax.rem(z + d, NZ) for d in range(1, NZ)]
-    at_high = [high * 2, (1 - high) * 2]
+    at_high = [high, 1 - high]
     at_core = [core, 1 - core]
 
-    def plane_device(dx, fl, fh, fc):
-        return at_high[fh] + at_core[fc], at_x[dx] + at_yl[fl] + z
+    def plane_device(dx, fl, fh):
+        return at_high[fh] * 2 + core, at_x[dx] + at_yl[fl] + z
+
+    sibling = (high * 2 + 1 - core, m)
 
     def z_device(dz):
         return c, m - z + at_z[dz]
@@ -106,6 +108,7 @@
     barrier = pltpu.get_barrier_semaphore()
     for dz in column:
         pl.semaphore_signal(barrier, inc=1, device_id=z_device(dz), device_id_type=MESH)
+    pl.semaphore_signal(barrier, inc=1, device_id=sibling, device_id_type=MESH)
     for d in plane:
         pl.semaphore_signal(barrier, inc=1, device_id=plane_device(*d), device_id_type=MESH)
 
@@ -148,12 +151,17 @@
         r = slice(r0, r0 + 32)
         make_field(r, turb_ref[r, :])
 
-    pl.semaphore_wait(barrier, len(plane) + NZ - 1)
-
-    near = [d for d in plane if d[2] == 0 and d[3] == 0]
+    pl.semaphore_wait(barrier, len(plane) + NZ)
+
+    near = [d for d in plane if d[2] == 0]
     for d in near:
         send(mod_a.at[xy], mod_a.at[xy], 0, plane_device(*d))
-    send(e_ref.at[pl.ds(0, PUPIL)], e_other.at[pl.ds(0, PUPIL)], FIELD, plane_device(0, 1, 1, 0))
+    send(e_ref.at[pl.ds(0, PUPIL)], e_other.at[pl.ds(0, PUPIL)], FIELD, plane_device(0, 1, 1))
+
+    recon_load.wait()
+    for j in range(5):
+        recon_t[0, j] = recon_ref[256 * j:256 * j + 256, :].T
+        send(recon_t.at[0, j], recon_t.at[1, j], RECON, sibling)
 
     lane = lax.broadcasted_iota(jnp.int32, (128, 128), 0)
     pix_load.wait()
@@ -188,9 +196,6 @@
         mod_b[z, j:j + 1, :] = mod_a[j]
     for dz in column:
         send(mod_b.at[z], mod_b.at[z], 1, z_device(dz))
-    recon_load.wait()
-    for i in range(10):
-        recon_t[:, 128 * i:128 * i + 128] = recon_ref[128 * i:128 * i + 128, :].T
     gt_load.wait()
     await_all(mod_b.at[pl.ds(0, NZ - 1)], 1)
 
@@ -285,35 +290,34 @@
         if step == STEPS - 1:
             frame_out[...] = frame
 
-        select_signals(frame, sig_buf.at[step, c])
+        select_signals(frame, sig_buf.at[step, high])
         base = 2 + 3 * step
         if step == 0:
-            other = at_high[1] + core
-            send(sig_buf.at[step, c], sig_buf.at[step, c], base, plane_device(0, 0, 0, 1))
             await_all(e_other.at[pl.ds(0, PUPIL)], FIELD)
             e_other[PUPIL:, 0:PUPIL] = -e_other[0:PUPIL, PUPIL:]
             e_other[PUPIL:, PUPIL:] = e_other[0:PUPIL, 0:PUPIL]
-            select_signals(compute_frame(e_other), sig_buf.at[step, other])
-            send(sig_buf.at[step, other], sig_buf.at[step, other], base, plane_device(0, 0, 0, 1))
-            await_all(sig_buf.at[step, pl.ds(0, 2)], base)
+            select_signals(compute_frame(e_other), sig_buf.at[step, at_high[1]])
+            await_all(recon_t.at[1], RECON)
         else:
-            for fh, fc in ((1, 1), (1, 0), (0, 1)):
-                send(sig_buf.at[step, c], sig_buf.at[step, c], base, plane_device(0, 0, fh, fc))
-            await_all(sig_buf.at[step, pl.ds(0, 3)], base)
-        signals = jnp.concatenate([sig_buf[step, k] for k in range(NCASE)], axis=0).astype(BF16)
-        part = jnp.dot(signals, recon_t[...], preferred_element_type=F32)
-        for k in range(NCASE):
-            rows = [part[k:k + 1, 640 * h:640 * h + 640] for h in range(2)]
-            part_bf[step, k] = jnp.concatenate(rows, axis=0).astype(BF16)
-        plane_buf[step, xy * NCASE + c] = part_bf[step, c]
+            send(sig_buf.at[step, high], sig_buf.at[step, high], base, plane_device(0, 0, 1))
+            await_all(sig_buf.at[step, pl.ds(0, 1)], base)
+
+        signals = jnp.concatenate([sig_buf[step, k] for k in range(2)], axis=0).astype(BF16)
+        for b in range(2):
+            part = jnp.concatenate(
+                [jnp.dot(signals, recon_t[b, j], preferred_element_type=F32) for j in range(5)], axis=1
+            )
+            for k in range(2):
+                rows = [part[k:k + 1, 640 * h:640 * h + 640] for h in range(2)]
+                part_bf[step, k, at_core[b]] = jnp.concatenate(rows, axis=0).astype(BF16)
+        plane_buf[step, xy * 2 + high] = part_bf[step, high]
         for d in plane:
-            device = plane_device(*d)
-            send(part_bf.at[step, device[0]], plane_buf.at[step, xy * NCASE + c], base + 1, device)
+            send(part_bf.at[step, at_high[d[2]]], plane_buf.at[step, xy * 2 + high], base + 1, plane_device(*d))
         await_all(plane_buf.at[step, pl.ds(0, len(plane))], base + 1)
         for k in range(NCASE):
-            acc = plane_buf[step, k].astype(F32)
+            acc = plane_buf[step, k // 2, k % 2].astype(F32)
             for j in range(1, NX * NYL):
-                acc = acc + plane_buf[step, j * NCASE + k].astype(F32)
+                acc = acc + plane_buf[step, j * 2 + k // 2, k % 2].astype(F32)
             tot_ref[step, 2 * k:2 * k + 2, :] = acc
         z_buf[step, z] = tot_ref[step].astype(BF16)
         for dz in column:
@@ -330,11 +334,13 @@
             for t in range(5):
                 cmd_out[pl.ds(t, 8, stride=5), :] = acc[:, 128 * t:128 * t + 128]
 
+    await_sent(recon_t.at[0], RECON)
     await_sent(mod_a.at[pl.ds(0, len(near))], 0)
     await_sent(mod_b.at[pl.ds(0, NZ - 1)], 1)
     for step in range(STEPS):
         base = 2 + 3 * step
-        await_sent(sig_buf.at[step, pl.ds(0, 2 + step)], base)
+        if step > 0:
+            await_sent(sig_buf.at[step, pl.ds(0, 1)], base)
         await_sent(plane_buf.at[step, pl.ds(0, len(plane))], base + 1)
         await_sent(z_buf.at[step, pl.ds(0, NZ - 1)], base + 2)
 
@@ -359,7 +365,7 @@
             pltpu.VMEM((PUPIL, 3 * AY), BF16),
             pltpu.VMEM((384, PUPIL), BF16),
             pltpu.VMEM((1280, 1024), BF16),
-            pltpu.VMEM((1024, 1280), BF16),
+            pltpu.VMEM((2, 5, 1024, 256), BF16),
             pltpu.VMEM((2, 8, PUPIL), F32),
             pltpu.VMEM((8, 1, 128), F32),
             pltpu.VMEM((8, 8, 128), F32),
@@ -373,16 +379,16 @@
             pltpu.VMEM((128, 1024), BF16),
             pltpu.VMEM((128, 5120), BF16),
             pltpu.VMEM((8, NF), F32),
-            pltpu.VMEM((STEPS, NCASE, 1, 1024), F32),
-            pltpu.VMEM((STEPS, NCASE, 2, 640), BF16),
-            pltpu.VMEM((STEPS, 32, 2, 640), BF16),
+            pltpu.VMEM((STEPS, 2, 1, 1024), F32),
+            pltpu.VMEM((STEPS, 2, 2, 2, 640), BF16),
+            pltpu.VMEM((STEPS, 16, 2, 2, 640), BF16),
             pltpu.VMEM((STEPS, 8, 640), F32),
             pltpu.VMEM((STEPS, NZ, 8, 640), BF16),
             pltpu.VMEM((40, 128), F32),
             pltpu.VMEM((64, 128), F32),
             pltpu.SemaphoreType.DMA((9,)),
-            pltpu.SemaphoreType.DMA((3 + 3 * STEPS,)),
-            pltpu.SemaphoreType.DMA((3 + 3 * STEPS,)),
+            pltpu.SemaphoreType.DMA((4 + 3 * STEPS,)),
+            pltpu.SemaphoreType.DMA((4 + 3 * STEPS,)),
         ],
         compiler_params=pltpu.CompilerParams(
             collective_id=0, has_side_effects=True, vmem_limit_bytes=60 * 1024 * 1024

time: 48.8 us -> 47.2 us (0.967)
  the two profiles are of different devices: /device:TPU:1 before, /device:TPU:4 now
where the time goes in v7:
time: 47.2 us; the launch traced here: 47 us
  Pallas kernels  44.5 us (94%)
  between operations  1.29 us (3%)
  local copies, waits for them, and re-layouts  1.21 us (3%)
    pallas_call x1, Pallas kernels, body(): pl.pallas_call(kernel, out_shape=(pltpu.VMEM((40, 128), F32), pltpu.VMEM(...  44.5 us
    unnamed x2, local copies, waits for them, and re-layouts  1.21 us

profile of v7, /device:TPU:4, one launch (start us, length us, event | category | flops | bytes accessed | tf_op | source)
XLA Modules:
  0.0 47.0 jit_solution(157502638926852414)
XLA Ops:
  1.3 44.5 %shard_map.113 = (f32[40,128]{1,0:T(8,128)S(1)}, f32[8,512]{1,0:T(8,128)S(1)}) custom-call(s32[1]{0:T(128)S(6)} %copy.16.mod_ref, f32[256,256]{1,0:T(8,128)} %bitcast.9, f32[256,256]{1,0:T(8,128)} %amp_hbm.1, s32[8,128]{1,0:T(8,128)} %bitcast.13, s32[40,128]{1,0:T(8,128)} %bitcast.12, f32[64,256]{1,0:T(8,128)} %bitcast.11, f32[80,256]{1,0:T(8,128)} %bitcast.10, ...), custom_call_target="tpu_custom_call" | custom-call | tf_op jit(solution)/shard_map/pallas_call | solution.py:352
  45.8 0.6 %copy.14 = f32[1,5120]{1,0:T(1,128)} copy(f32[1,5120]{1,0:T(1,128)S(1)} %bitcast.7) | data formatting | bytes 40960
  46.4 0.6 %copy.15 = f32[1,8,512]{2,1,0:T(8,128)} copy(f32[1,8,512]{2,1,0:T(8,128)S(1)} %bitcast.8) | data formatting | bytes 32768

commit v8 on v7

--- a/solution.py
+++ b/solution.py
@@ -20,7 +20,7 @@
 NX, NYL, NZ = 4, 2, 8
 NCASE = 4
 MESH = pl.DeviceIdType.MESH
-FIELD, RECON = 2 + 3 * STEPS, 3 + 3 * STEPS
+FIELD, RECON, LATE = 2 + 3 * STEPS, 3 + 3 * STEPS, 4 + 3 * STEPS
 F32 = jnp.float32
 BF16 = jnp.bfloat16
 
@@ -61,7 +61,7 @@
     cmd_out, frame_out,
     turb_ref, amp_ref, pix_ref, act_ref, gx_ref, gy_ref, gt_ref, gx_wide, gy_tall,
     recon_ref, recon_t, rows_ref, mod_a, mod_b, v_ref, l_ref, e_ref, e_other, x_ref, t_ref, y_ref,
-    oh_sig, oh_act, fr_ref, sig_buf, part_bf, plane_buf, tot_ref, z_buf, gat_ref, grid_ref,
+    oh_sig, oh_act, fr_ref, fr_other, sig_buf, part_bf, plane_buf, tot_ref, z_buf, gat_ref, grid_ref,
     local_sem, send_sem, recv_sem,
 ):
     c = lax.axis_index("case")
@@ -192,55 +192,63 @@
     gy_tall[256:256 + AX, :] = gy_low
 
     await_all(mod_a.at[pl.ds(0, len(near))], 0)
+    slots = {0: 0, 1: 1, 7: 2, 2: 3, 6: 4, 3: 5, 5: 6, 4: 7}
     for j in range(NX * NYL):
-        mod_b[z, j:j + 1, :] = mod_a[j]
+        mod_b[0, j:j + 1, :] = mod_a[j]
     for dz in column:
-        send(mod_b.at[z], mod_b.at[z], 1, z_device(dz))
+        send(mod_b.at[0], mod_b.at[slots[dz]], 1 if slots[dz] < 4 else LATE, z_device(dz))
     gt_load.wait()
-    await_all(mod_b.at[pl.ds(0, NZ - 1)], 1)
-
-    angle = (2.0 * math.pi / POINTS) * mod_b[...].reshape(64, 128)
-    ca, sa = sincos(angle)
-    centred = lax.broadcasted_iota(jnp.int32, (64, 128), 1).astype(F32)
+    centred = lax.broadcasted_iota(jnp.int32, (32, 128), 1).astype(F32)
     scale = 2.0 * math.pi * RADIUS / NF
-    rows_load.wait()
-    for h in range(2):
-        pos = scale * (centred + (128.0 * h - PUPIL // 2))
-        cols = slice(128 * h, 128 * h + 128)
-        vr, vi = sincos(pos * sa)
-        v_ref[0, :, cols] = vr
-        v_ref[1, :, cols] = vi
-        ur, ui = sincos(pos * ca)
-        for i in range(8):
-            mr = rows_ref[0, i:i + 1, cols]
-            mi = rows_ref[1, i:i + 1, cols]
-            l_ref[64 * i:64 * i + 64, cols] = (mr * ur - mi * ui).astype(BF16)
-            l_ref[64 * i:64 * i + 64, 128 * h + PUPIL:128 * h + PUPIL + 128] = (mr * ui + mi * ur).astype(BF16)
-
-    def compute_frame(field):
-        x_ref[...] = jnp.dot(l_ref[...], field[...], preferred_element_type=F32)
-        for i in range(8):
-            r = slice(64 * i, 64 * i + 64)
-            xr = x_ref[r, 0:PUPIL]
-            xi = x_ref[r, PUPIL:]
-            vr = v_ref[0]
-            vi = v_ref[1]
-            tr = xr * vr - xi * vi
-            ti = xr * vi + xi * vr
-            x_ref[r, 0:PUPIL] = tr
-            x_ref[r, PUPIL:] = ti
-            t_ref[r, :] = tr.astype(BF16)
-            t_ref[64 * i + 512:64 * i + 576, :] = ti.astype(BF16)
-        y_ref[...] = jnp.dot(t_ref[...], gt_ref[...], preferred_element_type=F32)
+
+    def modulate(part):
+        angle = (2.0 * math.pi / POINTS) * mod_b[4 * part:4 * part + 4].reshape(32, 128)
+        ca, sa = sincos(angle)
+        for h in range(2):
+            pos = scale * (centred + (128.0 * h - PUPIL // 2))
+            cols = slice(128 * h, 128 * h + 128)
+            vr, vi = sincos(pos * sa)
+            v_ref[0, 32 * part:32 * part + 32, cols] = vr
+            v_ref[1, 32 * part:32 * part + 32, cols] = vi
+            ur, ui = sincos(pos * ca)
+            for i in range(8):
+                mr = rows_ref[0, i:i + 1, cols]
+                mi = rows_ref[1, i:i + 1, cols]
+                r = slice(256 * part + 32 * i, 256 * part + 32 * i + 32)
+                l_ref[r, cols] = (mr * ur - mi * ui).astype(BF16)
+                l_ref[r, 128 * h + PUPIL:128 * h + PUPIL + 128] = (mr * ui + mi * ur).astype(BF16)
+
+    def compute_frame(field, out, parts, add):
+        points = slice(256 * parts[0], 256 * parts[-1] + 256)
+        x_ref[points, :] = jnp.dot(l_ref[points, :], field[...], preferred_element_type=F32)
+        for part in parts:
+            vr = v_ref[0, 32 * part:32 * part + 32, :]
+            vi = v_ref[1, 32 * part:32 * part + 32, :]
+            for i in range(8):
+                r = slice(256 * part + 32 * i, 256 * part + 32 * i + 32)
+                xr = x_ref[r, 0:PUPIL]
+                xi = x_ref[r, PUPIL:]
+                tr = xr * vr - xi * vi
+                ti = xr * vi + xi * vr
+                x_ref[r, 0:PUPIL] = tr
+                x_ref[r, PUPIL:] = ti
+                t_ref[512 * part + 32 * i:512 * part + 32 * i + 32, :] = tr.astype(BF16)
+                t_ref[512 * part + 32 * i + 256:512 * part + 32 * i + 288, :] = ti.astype(BF16)
+        both = slice(512 * parts[0], 512 * parts[-1] + 512)
+        y_ref[both, :] = jnp.dot(t_ref[both, :], gt_ref[...], preferred_element_type=F32)
         for i in range(8):
             for q in range(4):
                 cols = slice(128 * q, 128 * q + 128)
                 src = 128 * (1 - q % 2)
-                r = slice(64 * i, 64 * i + 64)
-                dr = x_ref[r, src:src + 128] - y_ref[64 * i + 512:64 * i + 576, cols]
-                di = x_ref[r, src + PUPIL:src + PUPIL + 128] + y_ref[r, cols]
-                fr_ref[i:i + 1, cols] = jnp.sum(dr * dr + di * di, axis=0, keepdims=True) * (1.0 / 256)
-        return fr_ref[...]
+                total = 0.0
+                for part in parts:
+                    r = slice(256 * part + 32 * i, 256 * part + 32 * i + 32)
+                    at = 512 * part + 32 * i
+                    dr = x_ref[r, src:src + 128] - y_ref[at + 256:at + 288, cols]
+                    di = x_ref[r, src + PUPIL:src + PUPIL + 128] + y_ref[at:at + 32, cols]
+                    total = total + (dr * dr + di * di)
+                row = jnp.sum(total, axis=0, keepdims=True) * (1.0 / 256)
+                out[i:i + 1, cols] = out[i:i + 1, cols] + row if add else row
 
     def select_signals(frame, slot):
         tiles = jnp.concatenate([frame[:, 128 * q:128 * q + 128] for q in range(4)], axis=0).astype(BF16)
@@ -286,19 +294,26 @@
                 r = slice(r0, r0 + 32)
                 make_field(r, turb_ref[r, :] - surface[r, :])
 
-        frame = compute_frame(e_ref)
-        if step == STEPS - 1:
-            frame_out[...] = frame
-
-        select_signals(frame, sig_buf.at[step, high])
         base = 2 + 3 * step
         if step == 0:
+            rows_load.wait()
+            await_all(mod_b.at[pl.ds(0, 3)], 1)
+            modulate(0)
+            compute_frame(e_ref, fr_ref, (0,), False)
             await_all(e_other.at[pl.ds(0, PUPIL)], FIELD)
             e_other[PUPIL:, 0:PUPIL] = -e_other[0:PUPIL, PUPIL:]
             e_other[PUPIL:, PUPIL:] = e_other[0:PUPIL, 0:PUPIL]
-            select_signals(compute_frame(e_other), sig_buf.at[step, at_high[1]])
+            compute_frame(e_other, fr_other, (0,), False)
+            await_all(mod_b.at[pl.ds(0, 4)], LATE)
+            modulate(1)
+            compute_frame(e_ref, fr_ref, (1,), True)
+            compute_frame(e_other, fr_other, (1,), True)
+            select_signals(fr_ref[...], sig_buf.at[step, high])
+            select_signals(fr_other[...], sig_buf.at[step, at_high[1]])
             await_all(recon_t.at[1], RECON)
         else:
+            compute_frame(e_ref, fr_ref, (0, 1), False)
+            select_signals(fr_ref[...], sig_buf.at[step, high])
             send(sig_buf.at[step, high], sig_buf.at[step, high], base, plane_device(0, 0, 1))
             await_all(sig_buf.at[step, pl.ds(0, 1)], base)
 
@@ -331,12 +346,14 @@
             acc = acc + tot_ref[step - 1]
         tot_ref[step] = acc
         if step == STEPS - 1:
+            frame_out[...] = fr_ref[...]
             for t in range(5):
                 cmd_out[pl.ds(t, 8, stride=5), :] = acc[:, 128 * t:128 * t + 128]
 
     await_sent(recon_t.at[0], RECON)
     await_sent(mod_a.at[pl.ds(0, len(near))], 0)
-    await_sent(mod_b.at[pl.ds(0, NZ - 1)], 1)
+    await_sent(mod_b.at[pl.ds(0, 3)], 1)
+    await_sent(mod_b.at[pl.ds(0, 4)], LATE)
     for step in range(STEPS):
         base = 2 + 3 * step
         if step > 0:
@@ -379,6 +396,7 @@
             pltpu.VMEM((128, 1024), BF16),
             pltpu.VMEM((128, 5120), BF16),
             pltpu.VMEM((8, NF), F32),
+            pltpu.VMEM((8, NF), F32),
             pltpu.VMEM((STEPS, 2, 1, 1024), F32),
             pltpu.VMEM((STEPS, 2, 2, 2, 640), BF16),
             pltpu.VMEM((STEPS, 16, 2, 2, 640), BF16),
@@ -387,8 +405,8 @@
             pltpu.VMEM((40, 128), F32),
             pltpu.VMEM((64, 128), F32),
             pltpu.SemaphoreType.DMA((9,)),
-            pltpu.SemaphoreType.DMA((4 + 3 * STEPS,)),
-            pltpu.SemaphoreType.DMA((4 + 3 * STEPS,)),
+            pltpu.SemaphoreType.DMA((5 + 3 * STEPS,)),
+            pltpu.SemaphoreType.DMA((5 + 3 * STEPS,)),
         ],
         compiler_params=pltpu.CompilerParams(
             collective_id=0, has_side_effects=True, vmem_limit_bytes=60 * 1024 * 1024

time: 47.2 us -> 46.9 us (level)
  no operation moved by 1% of the time
where the time goes in v8:
time: 46.9 us; the launch traced here: 46.6 us
  Pallas kernels  44.1 us (94%)
  between operations  1.29 us (3%)
  local copies, waits for them, and re-layouts  1.21 us (3%)
    pallas_call x1, Pallas kernels, body(): pl.pallas_call(kernel, out_shape=(pltpu.VMEM((40, 128), F32), pltpu.VMEM(...  44.1 us
    unnamed x2, local copies, waits for them, and re-layouts  1.21 us

profile of v8, /device:TPU:4, one launch (start us, length us, event | category | flops | bytes accessed | tf_op | source)
XLA Modules:
  0.0 46.6 jit_solution(15949589369636558583)
XLA Ops:
  1.3 44.1 %shard_map.113 = (f32[40,128]{1,0:T(8,128)S(1)}, f32[8,512]{1,0:T(8,128)S(1)}) custom-call(s32[1]{0:T(128)S(6)} %copy.16.mod_ref, f32[256,256]{1,0:T(8,128)} %bitcast.9, f32[256,256]{1,0:T(8,128)} %amp_hbm.1, s32[8,128]{1,0:T(8,128)} %bitcast.13, s32[40,128]{1,0:T(8,128)} %bitcast.12, f32[64,256]{1,0:T(8,128)} %bitcast.11, f32[80,256]{1,0:T(8,128)} %bitcast.10, ...), custom_call_target="tpu_custom_call" | custom-call | tf_op jit(solution)/shard_map/pallas_call | solution.py:369
  45.3 0.6 %copy.14 = f32[1,5120]{1,0:T(1,128)} copy(f32[1,5120]{1,0:T(1,128)S(1)} %bitcast.7) | data formatting | bytes 40960
  46.0 0.6 %copy.15 = f32[1,8,512]{2,1,0:T(8,128)} copy(f32[1,8,512]{2,1,0:T(8,128)S(1)} %bitcast.8) | data formatting | bytes 32768

commit v9 on v8

--- a/solution.py
+++ b/solution.py
@@ -20,7 +20,7 @@
 NX, NYL, NZ = 4, 2, 8
 NCASE = 4
 MESH = pl.DeviceIdType.MESH
-FIELD, RECON, LATE = 2 + 3 * STEPS, 3 + 3 * STEPS, 4 + 3 * STEPS
+FIELD, RECON, LATE, SCREEN, TOTAL = range(2 + 3 * STEPS, 7 + 3 * STEPS)
 F32 = jnp.float32
 BF16 = jnp.bfloat16
 
@@ -61,7 +61,7 @@
     cmd_out, frame_out,
     turb_ref, amp_ref, pix_ref, act_ref, gx_ref, gy_ref, gt_ref, gx_wide, gy_tall,
     recon_ref, recon_t, rows_ref, mod_a, mod_b, v_ref, l_ref, e_ref, e_other, x_ref, t_ref, y_ref,
-    oh_sig, oh_act, fr_ref, fr_other, sig_buf, part_bf, plane_buf, tot_ref, z_buf, gat_ref, grid_ref,
+    oh_sig, oh_act, fr_ref, fr_other, sig_buf, part_bf, plane_buf, tot_ref, tot_other, turb_other, z_buf, gat_ref, grid_ref,
     local_sem, send_sem, recv_sem,
 ):
     c = lax.axis_index("case")
@@ -134,22 +134,22 @@
 
     mod_a[xy] = jnp.full((1, 128), mod_ref[0], jnp.int32).astype(F32)
 
-    def make_field(r, phase):
+    def make_field(r, phase, field):
         cs, sn = sincos(phase)
         amp = amp_ref[r, :]
         er = (amp * cs).astype(BF16)
         ei = (amp * sn).astype(BF16)
         low = slice(r.start + PUPIL, r.stop + PUPIL)
-        e_ref[r, 0:PUPIL] = er
-        e_ref[r, PUPIL:] = ei
-        e_ref[low, 0:PUPIL] = -ei
-        e_ref[low, PUPIL:] = er
+        field[r, 0:PUPIL] = er
+        field[r, PUPIL:] = ei
+        field[low, 0:PUPIL] = -ei
+        field[low, PUPIL:] = er
 
     turb_load.wait()
     amp_load.wait()
     for r0 in range(0, PUPIL, 32):
         r = slice(r0, r0 + 32)
-        make_field(r, turb_ref[r, :])
+        make_field(r, turb_ref[r, :], e_ref)
 
     pl.semaphore_wait(barrier, len(plane) + NZ)
 
@@ -217,6 +217,36 @@
                 r = slice(256 * part + 32 * i, 256 * part + 32 * i + 32)
                 l_ref[r, cols] = (mr * ur - mi * ui).astype(BF16)
                 l_ref[r, 128 * h + PUPIL:128 * h + PUPIL + 128] = (mr * ui + mi * ur).astype(BF16)
+
+    def flatten_phase(total, screen, field):
+        stacked = jnp.concatenate([total[:, 128 * t:128 * t + 128] for t in range(5)], axis=0)
+        picked = jnp.dot(stacked.astype(BF16), oh_act[...], preferred_element_type=F32)
+        q_iota = lax.broadcasted_iota(jnp.int32, (40, 128), 0)
+        for s in range(40):
+            cols = slice(128 * s, 128 * s + 128)
+            block = picked[:, cols]
+            gat_ref[s:s + 1, :] = jnp.sum(jnp.where(q_iota == act_q[s:s + 1, :], block, 0.0), axis=0, keepdims=True)
+        for y8 in range(8):
+            s5, t = divmod(AX * y8, 128)
+            first = gat_ref[pl.ds(s5, 8, stride=5), :]
+            if t + AX <= 128:
+                row = first[:, t:t + AX]
+            else:
+                second = gat_ref[pl.ds(s5 + 1, 8, stride=5), :]
+                row = jnp.concatenate([first[:, t:], second[:, :t + AX - 128]], axis=1)
+            grid_ref[pl.ds(y8, 8, stride=8), :] = jnp.concatenate([row, jnp.zeros((8, 128 - AX), F32)], axis=1)
+        grid_high, grid_low = halves(grid_ref[...])
+        mapped = jnp.dot(
+            jnp.concatenate([grid_high, grid_low, grid_high], axis=1), gy_tall[...], preferred_element_type=F32
+        )
+        mapped_high, mapped_low = halves(mapped)
+        surface = jnp.dot(
+            gx_wide[...], jnp.concatenate([mapped_high, mapped_high, mapped_low], axis=0),
+            preferred_element_type=F32,
+        )
+        for r0 in range(0, PUPIL, 32):
+            r = slice(r0, r0 + 32)
+            make_field(r, screen[r, :] - surface[r, :], field)
 
     def compute_frame(field, out, parts, add):
         points = slice(256 * parts[0], 256 * parts[-1] + 256)
@@ -261,39 +291,6 @@
             )
 
     for step in range(STEPS):
-        if step > 0:
-            total = tot_ref[step - 1]
-            if step == 1:
-                await_sent(e_ref.at[pl.ds(0, PUPIL)], FIELD)
-            stacked = jnp.concatenate([total[:, 128 * t:128 * t + 128] for t in range(5)], axis=0)
-            picked = jnp.dot(stacked.astype(BF16), oh_act[...], preferred_element_type=F32)
-            q_iota = lax.broadcasted_iota(jnp.int32, (40, 128), 0)
-            for s in range(40):
-                cols = slice(128 * s, 128 * s + 128)
-                block = picked[:, cols]
-                gat_ref[s:s + 1, :] = jnp.sum(jnp.where(q_iota == act_q[s:s + 1, :], block, 0.0), axis=0, keepdims=True)
-            for y8 in range(8):
-                s5, t = divmod(AX * y8, 128)
-                first = gat_ref[pl.ds(s5, 8, stride=5), :]
-                if t + AX <= 128:
-                    row = first[:, t:t + AX]
-                else:
-                    second = gat_ref[pl.ds(s5 + 1, 8, stride=5), :]
-                    row = jnp.concatenate([first[:, t:], second[:, :t + AX - 128]], axis=1)
-                grid_ref[pl.ds(y8, 8, stride=8), :] = jnp.concatenate([row, jnp.zeros((8, 128 - AX), F32)], axis=1)
-            grid_high, grid_low = halves(grid_ref[...])
-            mapped = jnp.dot(
-                jnp.concatenate([grid_high, grid_low, grid_high], axis=1), gy_tall[...], preferred_element_type=F32
-            )
-            mapped_high, mapped_low = halves(mapped)
-            surface = jnp.dot(
-                gx_wide[...], jnp.concatenate([mapped_high, mapped_high, mapped_low], axis=0),
-                preferred_element_type=F32,
-            )
-            for r0 in range(0, PUPIL, 32):
-                r = slice(r0, r0 + 32)
-                make_field(r, turb_ref[r, :] - surface[r, :])
-
         base = 2 + 3 * step
         if step == 0:
             rows_load.wait()
@@ -312,10 +309,15 @@
             select_signals(fr_other[...], sig_buf.at[step, at_high[1]])
             await_all(recon_t.at[1], RECON)
         else:
+            await_sent(e_ref.at[pl.ds(0, PUPIL)], FIELD)
+            flatten_phase(tot_ref[0], turb_ref, e_ref)
             compute_frame(e_ref, fr_ref, (0, 1), False)
             select_signals(fr_ref[...], sig_buf.at[step, high])
-            send(sig_buf.at[step, high], sig_buf.at[step, high], base, plane_device(0, 0, 1))
-            await_all(sig_buf.at[step, pl.ds(0, 1)], base)
+            await_all(turb_other, SCREEN)
+            await_all(tot_other, TOTAL)
+            flatten_phase(tot_other[...], turb_other, e_other)
+            compute_frame(e_other, fr_other, (0, 1), False)
+            select_signals(fr_other[...], sig_buf.at[step, at_high[1]])
 
         signals = jnp.concatenate([sig_buf[step, k] for k in range(2)], axis=0).astype(BF16)
         for b in range(2):
@@ -337,6 +339,8 @@
         z_buf[step, z] = tot_ref[step].astype(BF16)
         for dz in column:
             send(z_buf.at[step, z], z_buf.at[step, z], base + 2, z_device(dz))
+        if step == 0:
+            send(turb_ref, turb_other, SCREEN, plane_device(0, 1, 1))
         await_all(z_buf.at[step, pl.ds(0, NZ - 1)], base + 2)
         acc = z_buf[step, 0].astype(F32)
         for j in range(1, NZ):
@@ -345,19 +349,21 @@
         if step > 0:
             acc = acc + tot_ref[step - 1]
         tot_ref[step] = acc
+        if step == 0:
+            send(tot_ref.at[0], tot_other, TOTAL, plane_device(0, 1, 1))
         if step == STEPS - 1:
             frame_out[...] = fr_ref[...]
             for t in range(5):
                 cmd_out[pl.ds(t, 8, stride=5), :] = acc[:, 128 * t:128 * t + 128]
 
     await_sent(recon_t.at[0], RECON)
+    await_sent(turb_ref, SCREEN)
+    await_sent(tot_ref.at[0], TOTAL)
     await_sent(mod_a.at[pl.ds(0, len(near))], 0)
     await_sent(mod_b.at[pl.ds(0, 3)], 1)
     await_sent(mod_b.at[pl.ds(0, 4)], LATE)
     for step in range(STEPS):
         base = 2 + 3 * step
-        if step > 0:
-            await_sent(sig_buf.at[step, pl.ds(0, 1)], base)
         await_sent(plane_buf.at[step, pl.ds(0, len(plane))], base + 1)
         await_sent(z_buf.at[step, pl.ds(0, NZ - 1)], base + 2)
 
@@ -401,12 +407,14 @@
             pltpu.VMEM((STEPS, 2, 2, 2, 640), BF16),
             pltpu.VMEM((STEPS, 16, 2, 2, 640), BF16),
             pltpu.VMEM((STEPS, 8, 640), F32),
+            pltpu.VMEM((8, 640), F32),
+            pltpu.VMEM((PUPIL, PUPIL), F32),
             pltpu.VMEM((STEPS, NZ, 8, 640), BF16),
             pltpu.VMEM((40, 128), F32),
             pltpu.VMEM((64, 128), F32),
             pltpu.SemaphoreType.DMA((9,)),
-            pltpu.SemaphoreType.DMA((5 + 3 * STEPS,)),
-            pltpu.SemaphoreType.DMA((5 + 3 * STEPS,)),
+            pltpu.SemaphoreType.DMA((7 + 3 * STEPS,)),
+            pltpu.SemaphoreType.DMA((7 + 3 * STEPS,)),
         ],
         compiler_params=pltpu.CompilerParams(
             collective_id=0, has_side_effects=True, vmem_limit_bytes=60 * 1024 * 1024

time: 46.9 us -> 47 us (level)
  no operation moved by 1% of the time
where the time goes in v9:
time: 47 us; the launch traced here: 46.7 us
  Pallas kernels  44.2 us (94%)
  between operations  1.29 us (3%)
  local copies, waits for them, and re-layouts  1.21 us (3%)
    pallas_call x1, Pallas kernels, body(): pl.pallas_call(kernel, out_shape=(pltpu.VMEM((40, 128), F32), pltpu.VMEM(...  44.2 us
    unnamed x2, local copies, waits for them, and re-layouts  1.21 us

profile of v9, /device:TPU:4, one launch (start us, length us, event | category | flops | bytes accessed | tf_op | source)
XLA Modules:
  0.0 46.7 jit_solution(18352113665910236107)
XLA Ops:
  1.3 44.2 %shard_map.113 = (f32[40,128]{1,0:T(8,128)S(1)}, f32[8,512]{1,0:T(8,128)S(1)}) custom-call(s32[1]{0:T(128)S(6)} %copy.16.mod_ref, f32[256,256]{1,0:T(8,128)} %bitcast.9, f32[256,256]{1,0:T(8,128)} %amp_hbm.1, s32[8,128]{1,0:T(8,128)} %bitcast.13, s32[40,128]{1,0:T(8,128)} %bitcast.12, f32[64,256]{1,0:T(8,128)} %bitcast.11, f32[80,256]{1,0:T(8,128)} %bitcast.10, ...), custom_call_target="tpu_custom_call" | custom-call | tf_op jit(solution)/shard_map/pallas_call | solution.py:375
  45.4 0.6 %copy.14 = f32[1,5120]{1,0:T(1,128)} copy(f32[1,5120]{1,0:T(1,128)S(1)} %bitcast.7) | data formatting | bytes 40960
  46.0 0.6 %copy.15 = f32[1,8,512]{2,1,0:T(8,128)} copy(f32[1,8,512]{2,1,0:T(8,128)S(1)} %bitcast.8) | data formatting | bytes 32768

commit v10 on v8

--- a/solution.py
+++ b/solution.py
@@ -315,19 +315,23 @@
             compute_frame(e_ref, fr_ref, (0, 1), False)
             select_signals(fr_ref[...], sig_buf.at[step, high])
             send(sig_buf.at[step, high], sig_buf.at[step, high], base, plane_device(0, 0, 1))
-            await_all(sig_buf.at[step, pl.ds(0, 1)], base)
-
-        signals = jnp.concatenate([sig_buf[step, k] for k in range(2)], axis=0).astype(BF16)
-        for b in range(2):
-            part = jnp.concatenate(
-                [jnp.dot(signals, recon_t[b, j], preferred_element_type=F32) for j in range(5)], axis=1
-            )
-            for k in range(2):
-                rows = [part[k:k + 1, 640 * h:640 * h + 640] for h in range(2)]
-                part_bf[step, k, at_core[b]] = jnp.concatenate(rows, axis=0).astype(BF16)
-        plane_buf[step, xy * 2 + high] = part_bf[step, high]
-        for d in plane:
-            send(part_bf.at[step, at_high[d[2]]], plane_buf.at[step, xy * 2 + high], base + 1, plane_device(*d))
+
+        for turn in (((0, 1),), ((0,), (1,)))[min(step, 1)]:
+            if turn == (1,):
+                await_all(sig_buf.at[step, pl.ds(0, 1)], base)
+            signals = jnp.concatenate([sig_buf[step, at_high[k]] for k in turn], axis=0).astype(BF16)
+            for b in range(2):
+                part = jnp.concatenate(
+                    [jnp.dot(signals, recon_t[b, j], preferred_element_type=F32) for j in range(5)], axis=1
+                )
+                for n, k in enumerate(turn):
+                    rows = [part[n:n + 1, 640 * h:640 * h + 640] for h in range(2)]
+                    part_bf[step, at_high[k], at_core[b]] = jnp.concatenate(rows, axis=0).astype(BF16)
+            if 0 in turn:
+                plane_buf[step, xy * 2 + high] = part_bf[step, high]
+            for d in plane:
+                if d[2] in turn:
+                    send(part_bf.at[step, at_high[d[2]]], plane_buf.at[step, xy * 2 + high], base + 1, plane_device(*d))
         await_all(plane_buf.at[step, pl.ds(0, len(plane))], base + 1)
         for k in range(NCASE):
             acc = plane_buf[step, k // 2, k % 2].astype(F32)

time: 46.9 us -> 46.9 us (level)
  no operation moved by 1% of the time
where the time goes in v10:
time: 46.9 us; the launch traced here: 46.6 us
  Pallas kernels  44.1 us (94%)
  between operations  1.29 us (3%)
  local copies, waits for them, and re-layouts  1.21 us (3%)
    pallas_call x1, Pallas kernels, body(): pl.pallas_call(kernel, out_shape=(pltpu.VMEM((40, 128), F32), pltpu.VMEM(...  44.1 us
    unnamed x2, local copies, waits for them, and re-layouts  1.21 us

profile of v10, /device:TPU:4, one launch (start us, length us, event | category | flops | bytes accessed | tf_op | source)
XLA Modules:
  0.0 46.6 jit_solution(4937262666038015201)
XLA Ops:
  1.3 44.1 %shard_map.113 = (f32[40,128]{1,0:T(8,128)S(1)}, f32[8,512]{1,0:T(8,128)S(1)}) custom-call(s32[1]{0:T(128)S(6)} %copy.16.mod_ref, f32[256,256]{1,0:T(8,128)} %bitcast.9, f32[256,256]{1,0:T(8,128)} %amp_hbm.1, s32[8,128]{1,0:T(8,128)} %bitcast.13, s32[40,128]{1,0:T(8,128)} %bitcast.12, f32[64,256]{1,0:T(8,128)} %bitcast.11, f32[80,256]{1,0:T(8,128)} %bitcast.10, ...), custom_call_target="tpu_custom_call" | custom-call | tf_op jit(solution)/shard_map/pallas_call | solution.py:373
  45.3 0.6 %copy.14 = f32[1,5120]{1,0:T(1,128)} copy(f32[1,5120]{1,0:T(1,128)S(1)} %bitcast.7) | data formatting | bytes 40960
  46.0 0.6 %copy.15 = f32[1,8,512]{2,1,0:T(8,128)} copy(f32[1,8,512]{2,1,0:T(8,128)S(1)} %bitcast.8) | data formatting | bytes 32768
